TPU v7x, 32 devices: a whole 2x2x4 slice. The times are simulated.
32 devices in a mesh: samp: 8 (over z, x), snp: 4 (over y, core).
Axes of the slice: x: 2, y: 2, z: 4, core: 2. Of those that a mesh axis runs over, the one named last changes fastest.
Arguments:
- genotype: bfloat16 [16384, 1024], P('samp', 'snp'), may hold values from -60 to 60
- phenotype: float32 [16384], P('samp'), may hold values from -6 to 6
- residual: float32 [16384], P('samp'), may hold values from -6 to 6
- sign_flips: int32 [16384, 127], P('samp'), may hold values from -1 to 1, as said below
- weights: bfloat16 [128, 49, 128], P('snp'), may hold values from -0.5 to 0.5
- member: int32 [128, 49], P('snp'), may hold values 0 or 1
- gene_start: int32 [128], P('snp'), may hold values from 0 to 1023, as said below
- gene_end: int32 [128], P('snp'), may hold values from 1 to 1024, as said below
Outputs:
- z_scores: float32 [128, 49, 128], P('snp')
Inputs may be any that keep to these rules, and one draw needn't show every extreme that they name: `sign_flips`: each entry is -1 or 1. `gene_start`: gene g's start lies among the SNPs of block g // 32 of 256 SNPs, at or past (g % 32) * (8) within it and before the next such mark, except that the last gene starts at 1023; the first gene starts at 0. gene_end - gene_start lies between 1 and 128 and reaches 128 in every block of genes except possibly the last; gene_end is at most 1024, and the last gene ends at 1024.
All inputs are finite; a program needn't handle non-finite values. No bound on the sum of `member` on one device may be relied on, other than what follows from the above.
Results may differ from a plain program's by a relative error of at most 0.0041.
Values may be sent and summed in bfloat16 or wider, within the bound.
A program may use at most 64 MiB of HBM per device.

v0:
```python
import functools

import jax
import jax.numpy as jnp
from jax import lax
from jax.experimental import pallas as pl
from jax.experimental.pallas import tpu as pltpu
from jax.sharding import PartitionSpec as P

MESH = pl.DeviceIdType.MESH
TILE = 16
PARTS = 4


def across(left, right):
    return lax.dot_general(left, right, (((0,), (0,)), ((), ())), preferred_element_type=jnp.float32)


def iotas(rows, cols):
    return (
        lax.broadcasted_iota(jnp.int32, (rows, cols), 0),
        lax.broadcasted_iota(jnp.int32, (rows, cols), 1),
    )


def share_of(rows, count):
    per = -(-rows // (count * TILE)) * TILE
    while rows % per:
        per += TILE
    return per


def columns_of(rows_ref):
    tiles, width = rows_ref.shape
    block = rows_ref[...]
    if tiles < width:
        block = jnp.concatenate([block, jnp.zeros((width - tiles, width), jnp.float32)], axis=0)
    return block.T


def sums_kernel(
    count, ring, window,
    geno, phen, resid, flips, starts, ends, member, weights,
    near_out, far_out, sums_out, corner_out, placed_out,
    geno_v, flips_v, halo_v, labels_v,
    early_s, early_r, early_p, early_g,
    late_s, late_r,
    tail_v, tail_sums, sums_s, sums_r, sums_t,
    load_sem, flip_sem, halo_ss, halo_rs,
    es_ss, es_rs, eg_ss, eg_rs, lt_ss, lt_rs,
    sm_ss, sm_rs, tl_ss, tl_rs,
):
    me = lax.axis_index("samp")
    mine = lax.axis_index("snp")
    before = lax.rem(mine + ring - 1, ring)
    after = lax.rem(mine + 1, ring)
    samples, snps = geno_v.shape
    blocks = snps // window
    part = samples // PARTS

    loads, flip_loads = [], []
    for i in range(PARTS):
        rows = pl.ds(i * part, part)
        loads.append(pltpu.make_async_copy(geno.at[rows], geno_v.at[rows], load_sem.at[i]))
        flip_loads.append(pltpu.make_async_copy(flips.at[rows], flips_v.at[rows], flip_sem.at[i]))
        loads[i].start()
        flip_loads[i].start()

    def peers(body):
        if count <= 16:
            for dist in range(1, count):
                body(dist)
        else:
            def step(dist, carry):
                body(dist)
                return carry
            lax.fori_loop(1, count, step, 0)

    def ahead(dist):
        return lax.rem(me + dist, count)

    def behind(dist):
        return lax.rem(me + count - dist, count)

    barrier = pltpu.get_barrier_semaphore()
    peers(lambda dist: pl.semaphore_signal(
        barrier, inc=1, device_id=(ahead(dist), mine), device_id_type=MESH))
    for other in (before, after):
        pl.semaphore_signal(barrier, inc=1, device_id=(me, other), device_id_type=MESH)

    flip_count = flips_v.shape[1]
    phen_cols = columns_of(phen)
    resid_cols = columns_of(resid)
    lanes = phen.shape[1]
    for i in range(PARTS):
        flip_loads[i].wait()
        for t in range(i * part // lanes, (i + 1) * part // lanes):
            rows = pl.ds(t * lanes, lanes)
            signs = flips_v[rows, :].astype(jnp.float32)
            labels_v[rows, pl.ds(0, flip_count)] = (signs * resid_cols[:, t:t + 1]).astype(jnp.bfloat16)
            labels_v[rows, pl.ds(flip_count, 1)] = phen_cols[:, t:t + 1].astype(jnp.bfloat16)

    pl.semaphore_wait(barrier, count + 1)

    def remote(src, dst, ss, rs, device):
        return pltpu.make_async_remote_copy(
            src_ref=src, dst_ref=dst, send_sem=ss, recv_sem=rs,
            device_id=device, device_id_type=MESH)

    halos = []
    for i in range(PARTS):
        rows = pl.ds(i * part, part)
        halos.append(remote(
            geno.at[rows, pl.ds(0, window)], halo_v.at[rows],
            halo_ss.at[i], halo_rs.at[i], (me, before)))
        halos[i].start()

    def guarded(owners, index, body):
        if owners == count:
            body()
        else:
            pl.when(index < owners)(body)

    def scatter_copy(buf, got, ss, rs, per, dist):
        start = pl.multiple_of(ahead(dist) * per, TILE)
        return remote(buf.at[pl.ds(start, per)], got.at[dist], ss.at[dist], rs.at[dist], (ahead(dist), mine))

    def gather_copy(piece, full, ss, rs, per, dist):
        start = pl.multiple_of(me * per, TILE)
        return remote(piece, full.at[pl.ds(start, per)], ss.at[dist], rs.at[dist], (ahead(dist), mine))

    def scatter_start(buf, got, ss, rs, per):
        owners = buf.shape[0] // per
        peers(lambda dist: guarded(
            owners, ahead(dist), lambda: scatter_copy(buf, got, ss, rs, per, dist).start()))

    def reduce_and_gather(buf, got, piece, full, ss, rs, gss, grs, per):
        owners = buf.shape[0] // per

        def owner():
            start = pl.multiple_of(me * per, TILE)
            rows = pl.ds(start, per)
            total = buf[rows, :].astype(jnp.float32)
            if count <= 16:
                for dist in range(1, count):
                    scatter_copy(buf, got, ss, rs, per, dist).wait_recv()
                    total += got[dist].astype(jnp.float32)
            else:
                def step(dist, total):
                    scatter_copy(buf, got, ss, rs, per, dist).wait_recv()
                    return total + got[dist].astype(jnp.float32)
                total = lax.fori_loop(1, count, step, total)
            piece[...] = total.astype(piece.dtype)
            peers(lambda dist: gather_copy(piece, full, gss, grs, per, dist).start())
            full[rows, :] = piece[...]
        guarded(owners, me, owner)

    def gather_wait(piece, full, gss, grs, per, low, high):
        def one(dist):
            start = pl.multiple_of(behind(dist) * per, TILE)

            @pl.when((behind(dist) >= low) & (behind(dist) < high))
            def _():
                remote(
                    piece, full.at[pl.ds(start, per)], gss.at[dist], grs.at[dist],
                    (ahead(dist), mine)).wait_recv()
        peers(one)

    def sends_wait(buf, got, piece, full, ss, rs, gss, grs, per):
        owners = buf.shape[0] // per
        peers(lambda dist: guarded(
            owners, ahead(dist), lambda: scatter_copy(buf, got, ss, rs, per, dist).wait_send()))
        guarded(owners, me, lambda: peers(
            lambda dist: gather_copy(piece, full, gss, grs, per, dist).wait_send()))

    for i in range(PARTS):
        loads[i].wait()
    own = geno_v[...]
    labels = labels_v[...]
    with_labels = across(own, labels)
    gram = across(own, own)
    ones = jnp.ones((8, samples), jnp.bfloat16)
    col_sums = jnp.dot(ones, own, preferred_element_type=jnp.float32)
    lab_sums = jnp.dot(ones, labels, preferred_element_type=jnp.float32)
    row8, _ = iotas(8, window)
    sums = jnp.where(row8 == blocks, lab_sums, 0.0)
    for b in range(blocks):
        sums = jnp.where(row8 == b, col_sums[:, b * window:(b + 1) * window], sums)
    sums_s[...] = sums

    def sums_copy(dist):
        return remote(sums_s, sums_r.at[dist], sm_ss.at[dist], sm_rs.at[dist], (ahead(dist), mine))

    row, col = iotas(window, window)
    for b in range(blocks):
        low, mid, high = b * window, (b + 1) * window, (b + 2) * window
        beyond = gram[low:mid, mid:high] if b < blocks - 1 else 0.0
        early_s[pl.ds(2 * low, window), :] = with_labels[low:mid].astype(jnp.bfloat16)
        band = jnp.where(col >= row, gram[low:mid, low:mid], beyond)
        early_s[pl.ds(2 * low + window, window), :] = band.astype(jnp.bfloat16)
    early_per = early_p.shape[0]
    scatter_start(early_s, early_r, es_ss, es_rs, early_per)
    peers(lambda dist: sums_copy(dist).start())

    place(mine * snps, starts, ends, member, weights, placed_out)
    reduce_and_gather(early_s, early_r, early_p, early_g, es_ss, es_rs, eg_ss, eg_rs, early_per)

    last = snps - window
    corner = jnp.zeros((window, window), jnp.float32)
    for i in range(PARTS):
        rows = pl.ds(i * part, part)
        halos[i].wait_recv()
        corner += across(geno_v[rows, pl.ds(last, window)], halo_v[rows, :])
    mid = window // 2
    half_row, half_col = iotas(mid, window)
    turned = pltpu.roll(corner, mid, 1)[:mid]
    folded = jnp.where(half_col - mid > half_row, corner.T[mid:], turned)
    late_s[...] = jnp.where(half_col < mid, corner[mid:], folded).astype(jnp.bfloat16)

    def late_copy(dist):
        return remote(late_s, late_r.at[dist], lt_ss.at[dist], lt_rs.at[dist], (ahead(dist), mine))

    peers(lambda dist: late_copy(dist).start())

    def collect(make, got, total):
        if count <= 16:
            for dist in range(1, count):
                make(dist).wait_recv()
                total += got[dist].astype(jnp.float32)
            return total

        def step(dist, total):
            make(dist).wait_recv()
            return total + got[dist].astype(jnp.float32)
        return lax.fori_loop(1, count, step, total)

    sums_t[...] = collect(sums_copy, sums_r, sums_s[...])
    tail_copies = [remote(sums_t, tail_sums, tl_ss.at[0], tl_rs.at[0], (me, before))]
    tail_copies[0].start()
    first_owners = 2 * window // early_per
    gather_wait(early_p, early_g, eg_ss, eg_rs, early_per, 0, first_owners)
    tail_copies.append(remote(
        early_g.at[pl.ds(0, 2 * window)], tail_v, tl_ss.at[1], tl_rs.at[1], (me, before)))
    tail_copies[1].start()
    gather_wait(early_p, early_g, eg_ss, eg_rs, early_per, first_owners, early_s.shape[0] // early_per)
    near_out[...] = early_g[...]
    sums_out[pl.ds(0, 8), :] = sums_t[...]

    folded = collect(late_copy, late_r, late_s[...].astype(jnp.float32))
    mirrored = jnp.concatenate([folded, folded], axis=0).T
    corner_out[pl.ds(0, mid), :] = pltpu.roll(folded, mid, 1)
    corner_out[pl.ds(mid, mid), :] = jnp.where(half_col < mid, folded, mirrored[mid:])

    for copy in tail_copies:
        copy.wait_recv()
    far_out[...] = tail_v[...]
    sums_out[pl.ds(8, 8), :] = tail_sums[...]

    for copy in halos + tail_copies:
        copy.wait_send()
    sends_wait(early_s, early_r, early_p, early_g, es_ss, es_rs, eg_ss, eg_rs, early_per)
    peers(lambda dist: sums_copy(dist).wait_send())
    peers(lambda dist: late_copy(dist).wait_send())


def place(offset, starts, ends, member, weights, placed):
    tissues, genes, window = weights.shape
    blocks = placed.shape[0]
    per_block = genes // blocks
    spacing = window // per_block
    gene_row, gene_col = iotas(genes, genes)

    def upright(row_ref):
        spread = jnp.broadcast_to(row_ref[...].astype(jnp.float32), (genes, genes))
        picked = jnp.where(gene_row == gene_col, spread, 0.0)
        return jnp.sum(picked, axis=1, keepdims=True).astype(jnp.int32)

    first, past = upright(starts), upright(ends)
    gene, lane = iotas(genes, window)
    inside = (lane < past - first).astype(jnp.float32)
    within = first - offset - (gene // per_block) * window
    extra = within - (gene % per_block) * spacing
    owned = member[...].astype(jnp.float32)
    for t in range(tissues):
        values = weights[t].astype(jnp.float32) * owned[:, t:t + 1] * inside
        bit = 1
        while bit < spacing:
            values = jnp.where((extra & bit) != 0, pltpu.roll(values, bit, 1), values)
            bit *= 2
        for b in range(blocks):
            genes_of = slice(b * per_block, (b + 1) * per_block)
            turned = pltpu.roll(values[genes_of], 0, 1, stride=spacing, stride_axis=0)
            kept = lane[genes_of] >= within[genes_of]
            rows = pl.ds(t * per_block, per_block)
            placed[b, rows, pl.ds(0, window)] = jnp.where(kept, turned, 0.0).astype(jnp.bfloat16)
            placed[b, rows, pl.ds(window, window)] = jnp.where(kept, 0.0, turned).astype(jnp.bfloat16)


def reduced_sums(genotype, phenotype, residual, sign_flips, starts, ends, member, weights):
    samples, snps = genotype.shape
    tissues, genes, window = weights.shape
    count, ring = lax.axis_size("samp"), lax.axis_size("snp")
    blocks = snps // window
    early_rows = 2 * snps
    early_per = share_of(early_rows, count)
    half, wide = jnp.bfloat16, jnp.float32
    dma = pltpu.SemaphoreType.DMA
    vmem = pl.BlockSpec(memory_space=pltpu.VMEM)
    hbm = pl.BlockSpec(memory_space=pl.ANY)
    return pl.pallas_call(
        functools.partial(sums_kernel, count, ring, window),
        out_shape=(
            jax.ShapeDtypeStruct((early_rows, window), half),
            jax.ShapeDtypeStruct((2 * window, window), half),
            jax.ShapeDtypeStruct((16, window), wide),
            jax.ShapeDtypeStruct((window, window), wide),
            jax.ShapeDtypeStruct((blocks, tissues * genes // blocks, 2 * window), half),
        ),
        in_specs=[hbm, vmem, vmem, hbm, vmem, vmem, vmem, vmem],
        out_specs=(vmem,) * 5,
        scratch_shapes=[
            pltpu.VMEM((samples, snps), half),
            pltpu.VMEM(sign_flips.shape, jnp.int32),
            pltpu.VMEM((samples, window), half),
            pltpu.VMEM((samples, window), half),
            pltpu.VMEM((early_rows, window), half),
            pltpu.VMEM((count, early_per, window), half),
            pltpu.VMEM((early_per, window), half),
            pltpu.VMEM((early_rows, window), half),
            pltpu.VMEM((window // 2, window), half),
            pltpu.VMEM((count, window // 2, window), half),
            pltpu.VMEM((2 * window, window), half),
            pltpu.VMEM((8, window), wide),
            pltpu.VMEM((8, window), wide),
            pltpu.VMEM((count, 8, window), wide),
            pltpu.VMEM((8, window), wide),
            dma((PARTS,)), dma((PARTS,)), dma((PARTS,)), dma((PARTS,)),
            dma((count,)), dma((count,)), dma((count,)), dma((count,)),
            dma((count,)), dma((count,)),
            dma((count,)), dma((count,)), dma((2,)), dma((2,)),
        ],
        compiler_params=pltpu.CompilerParams(collective_id=0, has_side_effects=True),
        name="sums",
    )(
        genotype, phenotype.reshape(-1, window), residual.reshape(-1, window), sign_flips,
        starts.reshape(1, genes), ends.reshape(1, genes), member, weights,
    )


def scores_kernel(sample_total, near, far, sums, corner, placed, out_hbm, out, sem):
    tissues, genes, window = out.shape
    blocks, rows_in_block, _ = placed.shape
    per_block = genes // blocks
    row, col = iotas(window, window)
    inverse = 1.0 / sample_total

    all_sums = jnp.concatenate([sums[...], jnp.zeros((window - 16, window), jnp.float32)], axis=0)
    by_column = all_sums.T
    lab_sum = all_sums[blocks:blocks + 1]

    def mean_row(b):
        at = b if b < blocks else 8
        return all_sums[at:at + 1] * inverse

    def mean_col(b):
        at = b if b < blocks else 8
        return by_column[:, at:at + 1] * inverse

    def block_at(b, band):
        ref, at = (near, 2 * b + band) if b < blocks else (far, band)
        return ref[pl.ds(at * window, window), :].astype(jnp.float32)

    def with_labels(b):
        centred = block_at(b, 0) - mean_col(b) * lab_sum
        centred = pltpu.roll(centred, 1, 1)
        high = centred.astype(jnp.bfloat16)
        low = (centred - high.astype(jnp.float32)).astype(jnp.bfloat16)
        return jnp.concatenate([high, low], axis=1)

    def diagonal(b):
        value = block_at(b, 1) * inverse - mean_col(b) * mean_row(b)
        return jnp.where(col > row, 2.0 * value, jnp.where(col == row, value, 0.0))

    def beside(b):
        products = block_at(b, 1) if b < blocks - 1 else corner[...]
        value = products * inverse - mean_col(b) * mean_row(b + 1)
        return jnp.where(col < row, 2.0 * value, 0.0)

    root = 1.0 / (sample_total ** 0.5)
    labelled = [with_labels(b) for b in range(blocks + 1)]
    pairs, bands = [], []
    for b in range(blocks):
        pairs.append(jnp.concatenate([labelled[b], labelled[b + 1]], axis=0))
        bands.append(jnp.concatenate([
            jnp.concatenate([diagonal(b), beside(b)], axis=1),
            jnp.concatenate([jnp.zeros((window, window), jnp.float32), diagonal(b + 1)], axis=1),
        ], axis=0).astype(jnp.bfloat16))

    copies = []
    step = next(n for n in range(min(7, tissues), 0, -1) if tissues % n == 0)
    for t in range(0, tissues, step):
        for b in range(blocks):
            half = placed[b, pl.ds(t * per_block, step * per_block), :]
            top = jnp.dot(half, pairs[b], preferred_element_type=jnp.float32)
            square = jnp.dot(half, bands[b], preferred_element_type=jnp.float32)
            variance = jnp.sum(square * half.astype(jnp.float32), axis=1, keepdims=True)
            scale = lax.rsqrt(jnp.maximum(variance, 0.0) + 1e-06) * root
            scores = (top[:, :window] + top[:, window:]) * scale
            out[pl.ds(t, step), pl.ds(b * per_block, per_block), :] = scores.reshape(step, per_block, window)
        part = pl.ds(t, step)
        copies.append(pltpu.make_async_copy(out.at[part], out_hbm.at[part], sem.at[t // step]))
        copies[-1].start()
    for copy in copies:
        copy.wait()


def on_device(genotype, phenotype, residual, sign_flips, weights, member, gene_start, gene_end):
    by_tissue = weights.transpose(1, 0, 2)
    near, far, sums, corner, placed = reduced_sums(
        genotype, phenotype, residual, sign_flips, gene_start, gene_end, member, by_tissue)
    vmem = pl.BlockSpec(memory_space=pltpu.VMEM)
    scores = pl.pallas_call(
        functools.partial(scores_kernel, genotype.shape[0] * lax.axis_size("samp")),
        out_shape=jax.ShapeDtypeStruct(by_tissue.shape, jnp.float32),
        in_specs=[vmem] * 5,
        out_specs=pl.BlockSpec(memory_space=pl.ANY),
        scratch_shapes=[
            pltpu.VMEM(by_tissue.shape, jnp.float32),
            pltpu.SemaphoreType.DMA((by_tissue.shape[0],)),
        ],
        name="scores",
    )(near, far, sums, corner, placed)
    return scores.transpose(1, 0, 2)


def solution(mesh):
    return jax.shard_map(
        on_device,
        mesh=mesh,
        in_specs=(
            P("samp", "snp"),
            P("samp"),
            P("samp"),
            P("samp", None),
            P("snp", None, None),
            P("snp", None),
            P("snp"),
            P("snp"),
        ),
        out_specs=P("snp", None, None),
        check_vma=False,
    )
```

profile of v0, /device:TPU:0, one launch (start us, length us, event | category | flops | bytes accessed | tf_op | source)
XLA Modules:
  0.0 23.9 jit_solution(14201085055868957118)
XLA Ops:
  0.0 20.6 %sums.1 = (bf16[512,128]{1,0:T(8,128)(2,1)}, bf16[256,128]{1,0:T(8,128)(2,1)}, f32[16,128]{1,0:T(8,128)}, f32[128,128]{1,0:T(8,128)}, bf16[2,784,256]{2,1,0:T(8,128)(2,1)}) custom-call(bf16[2048,256]{1,0:T(8,128)(2,1)} %geno.1, f32[16,128]{1,0:T(8,128)} %bitcast.7, f32[16,128]{1,0:T(8,128)} %bitcast.8, s32[2048,127]{1,0:T(8,128)} %flips.1, s32[1,32]{1,0:T(1,128)} %bitcast.9, ...), custom_call_target="tpu_custom_call" | custom-call | tf_op jit(solution)/shard_map/sums/pallas_call | solution.py:310
  20.6 3.3 %scores.1 = f32[49,32,128]{2,1,0:T(8,128)} custom-call(bf16[512,128]{1,0:T(8,128)(2,1)} %get-tuple-element.10.near, bf16[256,128]{1,0:T(8,128)(2,1)} %get-tuple-element.11.far, f32[16,128]{1,0:T(8,128)} %get-tuple-element.12.sums, f32[128,128]{1,0:T(8,128)} %get-tuple-element.13.corner, bf16[2,784,256]{2,1,0:T(8,128)(2,1)} %get-tuple-element.14.placed), custom_call_target="tpu_custom_call" | custom-call | tf_op jit(solution)/shard_map/scores/pallas_call | solution.py:422
where the time goes:
time: 24.3 us; the launch traced here: 23.9 us
  Pallas kernels  23.9 us (98%)
    pallas_call x1, Pallas kernels, reduced_sums(): pl.pallas_call(functools.partial(sums_kernel, count, ring, window), out_s...  20.6 us
    pallas_call x1, Pallas kernels, on_device(): pl.pallas_call(functools.partial(scores_kernel, genotype.shape[0] * lax.a...  3.31 us

commit v1 on v0

v1 whole, which is shorter than its diff:
```python
import functools

import jax
import jax.numpy as jnp
from jax import lax
from jax.experimental import pallas as pl
from jax.experimental.pallas import tpu as pltpu
from jax.sharding import PartitionSpec as P

MESH = pl.DeviceIdType.MESH
TILE = 16
PARTS = 4
VMEM_LIMIT = 24 * 1024 * 1024


def across(left, right):
    return lax.dot_general(left, right, (((0,), (0,)), ((), ())), preferred_element_type=jnp.float32)


def iotas(rows, cols):
    return (
        lax.broadcasted_iota(jnp.int32, (rows, cols), 0),
        lax.broadcasted_iota(jnp.int32, (rows, cols), 1),
    )


def share_of(rows, count):
    per = -(-rows // (count * TILE)) * TILE
    while rows % per:
        per += TILE
    return per


def square_of(rows):
    tiles, width = rows.shape
    return jnp.concatenate([rows, jnp.zeros((width - tiles, width), jnp.float32)], axis=0)


def sums_kernel(
    count, ring, window,
    geno, phen, resid, flips, starts, ends, member, weights,
    near_out, far_out, corner_out, placed_out,
    phen_v, resid_v, starts_v, ends_v, member_v, weights_v,
    geno_v, flips_v, halo_v, labels_v,
    main_s, main_r, main_p, main_g,
    corner_s, corner_r, corner_p, corner_g,
    tail_v, tail_sums, sums_s, sums_r, sums_t, cols_v,
    load_sem, flip_sem, small_sem, halo_ss, halo_rs,
    ms_ss, ms_rs, mg_ss, mg_rs, cs_ss, cs_rs, cg_ss, cg_rs,
    sm_ss, sm_rs, tl_ss, tl_rs,
):
    me = lax.axis_index("samp")
    mine = lax.axis_index("snp")
    has_before = mine > 0
    has_after = mine < ring - 1
    before = jnp.maximum(mine - 1, 0)
    after = jnp.minimum(mine + 1, ring - 1)
    samples, snps = geno_v.shape
    blocks = snps // window
    part = samples // PARTS
    owners, per = corner_g.shape[0], corner_g.shape[1]
    inverse = 1.0 / (samples * count)

    def peers(body):
        if count <= 16:
            for dist in range(1, count):
                body(dist)
        else:
            def step(dist, carry):
                body(dist)
                return carry
            lax.fori_loop(1, count, step, 0)

    def ahead(dist):
        return lax.rem(me + dist, count)

    def behind(dist):
        return lax.rem(me + count - dist, count)

    barrier = pltpu.get_barrier_semaphore()
    peers(lambda dist: pl.semaphore_signal(
        barrier, inc=1, device_id=(ahead(dist), mine), device_id_type=MESH))

    @pl.when(has_before)
    def _():
        pl.semaphore_signal(barrier, inc=1, device_id=(me, before), device_id_type=MESH)

    @pl.when(has_after)
    def _():
        pl.semaphore_signal(barrier, inc=1, device_id=(me, after), device_id_type=MESH)

    small = [
        pltpu.make_async_copy(src, dst, small_sem.at[i])
        for i, (src, dst) in enumerate((
            (resid, resid_v), (phen, phen_v), (starts, starts_v), (ends, ends_v),
            (member, member_v), (weights, weights_v),
        ))
    ]
    loads, flip_loads = [], []
    for copy in small[:2]:
        copy.start()
    for i in range(PARTS):
        rows = pl.ds(i * part, part)
        loads.append(pltpu.make_async_copy(geno.at[rows], geno_v.at[rows], load_sem.at[i]))
        flip_loads.append(pltpu.make_async_copy(flips.at[rows], flips_v.at[rows], flip_sem.at[i]))
        flip_loads[i].start()
        loads[i].start()
    for copy in small[2:]:
        copy.start()

    flip_count = flips_v.shape[1]
    for copy in small[:2]:
        copy.wait()
    phen_cols = square_of(phen_v[...]).T
    resid_cols = square_of(resid_v[...]).T
    lanes = phen_v.shape[1]
    for i in range(PARTS):
        flip_loads[i].wait()
        for t in range(i * part // lanes, (i + 1) * part // lanes):
            rows = pl.ds(t * lanes, lanes)
            signs = flips_v[rows, :].astype(jnp.float32)
            labels_v[rows, pl.ds(0, flip_count)] = (signs * resid_cols[:, t:t + 1]).astype(jnp.bfloat16)
            labels_v[rows, pl.ds(flip_count, 1)] = phen_cols[:, t:t + 1].astype(jnp.bfloat16)

    both = has_before & has_after

    @pl.when(both)
    def _():
        pl.semaphore_wait(barrier, count + 1)

    @pl.when(jnp.logical_not(both))
    def _():
        pl.semaphore_wait(barrier, count if ring > 1 else count - 1)

    def remote(src, dst, ss, rs, device):
        return pltpu.make_async_remote_copy(
            src_ref=src, dst_ref=dst, send_sem=ss, recv_sem=rs,
            device_id=device, device_id_type=MESH)

    halos = []
    for i in range(PARTS):
        rows = pl.ds(i * part, part)
        halos.append(remote(
            geno.at[rows, pl.ds(0, window)], halo_v.at[rows],
            halo_ss.at[i], halo_rs.at[i], (me, before)))

    @pl.when(has_before)
    def _():
        for copy in halos:
            copy.start()

    def guarded(index, body):
        if owners == count:
            body()
        else:
            pl.when(index < owners)(body)

    class Exchange:
        def __init__(self, send, got, piece, full, ss, rs, gss, grs):
            self.send, self.got, self.piece, self.full = send, got, piece, full
            self.ss, self.rs, self.gss, self.grs = ss, rs, gss, grs

        def scatter_copy(self, dist):
            return remote(
                self.send.at[ahead(dist)], self.got.at[dist],
                self.ss.at[dist], self.rs.at[dist], (ahead(dist), mine))

        def gather_copy(self, dist, slot):
            return remote(
                self.piece, self.full.at[slot],
                self.gss.at[dist], self.grs.at[dist], (ahead(dist), mine))

        def scatter(self):
            peers(lambda dist: guarded(ahead(dist), lambda: self.scatter_copy(dist).start()))

        def reduce(self, finish):
            def owner():
                total = self.send[me].astype(jnp.float32)
                if count <= 16:
                    for dist in range(1, count):
                        self.scatter_copy(dist).wait_recv()
                        total += self.got[dist].astype(jnp.float32)
                else:
                    def step(dist, total):
                        self.scatter_copy(dist).wait_recv()
                        return total + self.got[dist].astype(jnp.float32)
                    total = lax.fori_loop(1, count, step, total)
                self.piece[...] = finish(total).astype(self.piece.dtype)
                peers(lambda dist: self.gather_copy(dist, me).start())
                self.full[me] = self.piece[...]
            guarded(me, owner)

        def gather_wait(self):
            peers(lambda dist: guarded(
                behind(dist), lambda: self.gather_copy(dist, behind(dist)).wait_recv()))

        def sends_wait(self):
            peers(lambda dist: guarded(ahead(dist), lambda: self.scatter_copy(dist).wait_send()))
            guarded(me, lambda: peers(lambda dist: self.gather_copy(dist, me).wait_send()))

    main = [
        Exchange(
            main_s.at[b], main_r.at[b], main_p.at[b], main_g.at[b],
            ms_ss.at[b], ms_rs.at[b], mg_ss.at[b], mg_rs.at[b])
        for b in range(blocks)
    ]
    edge = Exchange(corner_s, corner_r, corner_p, corner_g, cs_ss, cs_rs, cg_ss, cg_rs)

    for i in range(PARTS):
        loads[i].wait()
    own = geno_v[...]
    labels = labels_v[...]
    with_labels = across(own, labels)
    gram = across(own, own)
    ones = jnp.ones((8, samples), jnp.bfloat16)
    col_sums = jnp.dot(ones, own, preferred_element_type=jnp.float32)
    lab_sums = jnp.dot(ones, labels, preferred_element_type=jnp.float32)
    row8, _ = iotas(8, window)
    sums = jnp.where(row8 == blocks, lab_sums, 0.0)
    for b in range(blocks):
        sums = jnp.where(row8 == b, col_sums[:, b * window:(b + 1) * window], sums)
    sums_s[...] = sums

    def sums_copy(dist):
        return remote(sums_s, sums_r.at[dist], sm_ss.at[dist], sm_rs.at[dist], (ahead(dist), mine))

    peers(lambda dist: sums_copy(dist).start())
    row, col = iotas(window, window)
    for b in range(blocks):
        low, mid, high = b * window, (b + 1) * window, (b + 2) * window
        beyond = gram[low:mid, mid:high] if b < blocks - 1 else 0.0
        band = jnp.where(col >= row, gram[low:mid, low:mid], beyond)
        main_s[b, :, pl.ds(0, per), :] = with_labels[low:mid].astype(jnp.bfloat16).reshape(owners, per, window)
        main_s[b, :, pl.ds(per, per), :] = band.astype(jnp.bfloat16).reshape(owners, per, window)
        main[b].scatter()

    for copy in small[2:]:
        copy.wait()
    place(mine * snps, starts_v, ends_v, member_v, weights_v, placed_out)

    total = sums_s[...]
    if count <= 16:
        for dist in range(1, count):
            sums_copy(dist).wait_recv()
            total += sums_r[dist]
    else:
        def step(dist, total):
            sums_copy(dist).wait_recv()
            return total + sums_r[dist]
        total = lax.fori_loop(1, count, step, total)
    sums_t[...] = total
    cols_v[...] = square_of(total).T
    tail_copies = [remote(sums_t, tail_sums, tl_ss.at[0], tl_rs.at[0], (me, before))]

    @pl.when(has_before)
    def _():
        tail_copies[0].start()

    my_rows = pl.ds(pl.multiple_of(me * per, per), per) if owners == count else pl.ds(
        pl.multiple_of(jnp.minimum(me, owners - 1) * per, per), per)
    row_of, col_of = iotas(per, window)
    row_of = row_of + me * per

    def mean_col(b):
        return cols_v[my_rows, :][:, b:b + 1] * inverse

    def finish_main(b):
        def finish(total):
            at = mean_col(b)
            scored = total[:per] - at * sums_t[blocks:blocks + 1, :]
            scored = pltpu.roll(scored, 1, 1)
            mean_row = sums_t[b:b + 1, :] * inverse
            if b < blocks - 1:
                mean_row = jnp.where(col_of >= row_of, mean_row, sums_t[b + 1:b + 2, :] * inverse)
            value = total[per:] * inverse - at * mean_row
            value = jnp.where(col_of == row_of, value, 2.0 * value)
            if b == blocks - 1:
                value = jnp.where(col_of >= row_of, value, 0.0)
            return jnp.concatenate([scored, value], axis=0)
        return finish

    for b in range(blocks):
        main[b].reduce(finish_main(b))

    last = snps - window

    @pl.when(has_after)
    def _():
        corner = jnp.zeros((window, window), jnp.float32)
        for i in range(PARTS):
            rows = pl.ds(i * part, part)
            halos[i].wait_recv()
            corner += across(geno_v[rows, pl.ds(last, window)], halo_v[rows, :])
        corner_s[...] = corner.astype(jnp.bfloat16).reshape(owners, per, window)
        edge.scatter()

    main[0].gather_wait()
    tail_copies.append(remote(main_g.at[0], tail_v, tl_ss.at[1], tl_rs.at[1], (me, before)))

    @pl.when(has_before)
    def _():
        tail_copies[1].start()

    def finish_edge(total):
        value = total * inverse - mean_col(blocks - 1) * (tail_sums[0:1, :] * inverse)
        return jnp.where(col_of < row_of, 2.0 * value, 0.0)

    @pl.when(has_after)
    def _():
        tail_copies[0].wait_recv()
        edge.reduce(finish_edge)

    for b in range(1, blocks):
        main[b].gather_wait()
    near_out[...] = main_g[...]

    @pl.when(has_after)
    def _():
        edge.gather_wait()
        corner_out[...] = corner_g[...]
        tail_copies[1].wait_recv()
        far_out[...] = tail_v[...]

    @pl.when(jnp.logical_not(has_after))
    def _():
        corner_out[...] = jnp.zeros_like(corner_out)
        far_out[...] = jnp.zeros_like(far_out)

    @pl.when(has_before)
    def _():
        for copy in halos + tail_copies:
            copy.wait_send()
    peers(lambda dist: sums_copy(dist).wait_send())
    for exchange in main:
        exchange.sends_wait()
    pl.when(has_after)(edge.sends_wait)


def place(offset, starts, ends, member, weights, placed):
    tissues, genes, window = weights.shape
    blocks = placed.shape[0]
    per_block = genes // blocks
    spacing = window // per_block
    gene_row, gene_col = iotas(genes, genes)

    def upright(row_ref):
        spread = jnp.broadcast_to(row_ref[...].astype(jnp.float32), (genes, genes))
        picked = jnp.where(gene_row == gene_col, spread, 0.0)
        return jnp.sum(picked, axis=1, keepdims=True).astype(jnp.int32)

    first, past = upright(starts), upright(ends)
    gene, lane = iotas(genes, window)
    inside = (lane < past - first).astype(jnp.float32)
    within = first - offset - (gene // per_block) * window
    extra = within - (gene % per_block) * spacing
    owned = member[...].astype(jnp.float32)
    for t in range(tissues):
        values = weights[t].astype(jnp.float32) * owned[:, t:t + 1] * inside
        bit = 1
        while bit < spacing:
            values = jnp.where((extra & bit) != 0, pltpu.roll(values, bit, 1), values)
            bit *= 2
        for b in range(blocks):
            genes_of = slice(b * per_block, (b + 1) * per_block)
            turned = pltpu.roll(values[genes_of], 0, 1, stride=spacing, stride_axis=0)
            kept = lane[genes_of] >= within[genes_of]
            rows = pl.ds(t * per_block, per_block)
            placed[b, rows, pl.ds(0, window)] = jnp.where(kept, turned, 0.0).astype(jnp.bfloat16)
            placed[b, rows, pl.ds(window, window)] = jnp.where(kept, 0.0, turned).astype(jnp.bfloat16)


def reduced_sums(genotype, phenotype, residual, sign_flips, starts, ends, member, weights):
    samples, snps = genotype.shape
    tissues, genes, window = weights.shape
    count, ring = lax.axis_size("samp"), lax.axis_size("snp")
    blocks = snps // window
    per = share_of(window, count)
    owners = window // per
    half, wide = jnp.bfloat16, jnp.float32
    dma = pltpu.SemaphoreType.DMA
    vmem = pl.BlockSpec(memory_space=pltpu.VMEM)
    hbm = pl.BlockSpec(memory_space=pltpu.HBM)
    operands = (
        genotype, phenotype.reshape(-1, window), residual.reshape(-1, window), sign_flips,
        starts.reshape(1, genes), ends.reshape(1, genes), member, weights,
    )
    return pl.pallas_call(
        functools.partial(sums_kernel, count, ring, window),
        out_shape=(
            jax.ShapeDtypeStruct((blocks, owners, 2 * per, window), half),
            jax.ShapeDtypeStruct((owners, 2 * per, window), half),
            jax.ShapeDtypeStruct((owners, per, window), half),
            jax.ShapeDtypeStruct((blocks, tissues * genes // blocks, 2 * window), half),
        ),
        in_specs=[hbm] * 8,
        out_specs=(vmem,) * 4,
        scratch_shapes=[pltpu.VMEM(x.shape, x.dtype) for x in operands[1:3] + operands[4:]] + [
            pltpu.VMEM((samples, snps), half),
            pltpu.VMEM(sign_flips.shape, jnp.int32),
            pltpu.VMEM((samples, window), half),
            pltpu.VMEM((samples, window), half),
            pltpu.VMEM((blocks, owners, 2 * per, window), half),
            pltpu.VMEM((blocks, count, 2 * per, window), half),
            pltpu.VMEM((blocks, 2 * per, window), half),
            pltpu.VMEM((blocks, owners, 2 * per, window), half),
            pltpu.VMEM((owners, per, window), half),
            pltpu.VMEM((count, per, window), half),
            pltpu.VMEM((per, window), half),
            pltpu.VMEM((owners, per, window), half),
            pltpu.VMEM((owners, 2 * per, window), half),
            pltpu.VMEM((8, window), wide),
            pltpu.VMEM((8, window), wide),
            pltpu.VMEM((count, 8, window), wide),
            pltpu.VMEM((8, window), wide),
            pltpu.VMEM((window, window), wide),
            dma((PARTS,)), dma((PARTS,)), dma((6,)), dma((PARTS,)), dma((PARTS,)),
            dma((blocks, count)), dma((blocks, count)), dma((blocks, count)), dma((blocks, count)),
            dma((count,)), dma((count,)), dma((count,)), dma((count,)),
            dma((count,)), dma((count,)), dma((2,)), dma((2,)),
        ],
        compiler_params=pltpu.CompilerParams(
            collective_id=0, has_side_effects=True, vmem_limit_bytes=VMEM_LIMIT),
        name="sums",
    )(*(pltpu.with_memory_space_constraint(x, pltpu.HBM) for x in operands))


def scores_kernel(sample_total, near, far, corner, placed, out_hbm, out, sem):
    tissues, genes, window = out.shape
    blocks = placed.shape[0]
    per_block = genes // blocks
    per = corner.shape[1]
    row, col = iotas(window, window)
    root = 1.0 / (sample_total ** 0.5)

    def piece(ref, at):
        return ref[:, pl.ds(at, per), :].reshape(window, window)

    def source(b):
        return near.at[b] if b < blocks else far

    def masked(keep, value):
        return jnp.where(keep, value.astype(jnp.float32), 0.0).astype(jnp.bfloat16)

    labelled = [piece(source(b), 0) for b in range(blocks + 1)]
    banded = [piece(source(b), per) for b in range(blocks + 1)]
    diagonal = [masked(col >= row, band) for band in banded]
    beside = [masked(col < row, band) for band in banded[:blocks - 1]] + [piece(corner, 0)]
    nothing = jnp.zeros((window, window), jnp.bfloat16)
    pairs, bands = [], []
    for b in range(blocks):
        pairs.append(jnp.concatenate([labelled[b], labelled[b + 1]], axis=0))
        bands.append(jnp.concatenate([
            jnp.concatenate([diagonal[b], beside[b]], axis=1),
            jnp.concatenate([nothing, diagonal[b + 1]], axis=1),
        ], axis=0))

    copies = []
    step = next(n for n in range(min(7, tissues), 0, -1) if tissues % n == 0)
    for t in range(0, tissues, step):
        for b in range(blocks):
            half = placed[b, pl.ds(t * per_block, step * per_block), :]
            top = jnp.dot(half, pairs[b], preferred_element_type=jnp.float32)
            square = jnp.dot(half, bands[b], preferred_element_type=jnp.float32)
            variance = jnp.sum(square * half.astype(jnp.float32), axis=1, keepdims=True)
            scale = lax.rsqrt(jnp.maximum(variance, 0.0) + 1e-06) * root
            out[pl.ds(t, step), pl.ds(b * per_block, per_block), :] = (top * scale).reshape(step, per_block, window)
        part = pl.ds(t, step)
        copies.append(pltpu.make_async_copy(out.at[part], out_hbm.at[part], sem.at[t // step]))
        copies[-1].start()
    for copy in copies:
        copy.wait()


def on_device(genotype, phenotype, residual, sign_flips, weights, member, gene_start, gene_end):
    by_tissue = weights.transpose(1, 0, 2)
    near, far, corner, placed = reduced_sums(
        genotype, phenotype, residual, sign_flips, gene_start, gene_end, member, by_tissue)
    vmem = pl.BlockSpec(memory_space=pltpu.VMEM)
    scores = pl.pallas_call(
        functools.partial(scores_kernel, genotype.shape[0] * lax.axis_size("samp")),
        out_shape=jax.ShapeDtypeStruct(by_tissue.shape, jnp.float32),
        in_specs=[vmem] * 4,
        out_specs=pl.BlockSpec(memory_space=pltpu.HBM),
        scratch_shapes=[
            pltpu.VMEM(by_tissue.shape, jnp.float32),
            pltpu.SemaphoreType.DMA((by_tissue.shape[0],)),
        ],
        compiler_params=pltpu.CompilerParams(vmem_limit_bytes=VMEM_LIMIT),
        name="scores",
    )(near, far, corner, placed)
    return scores.transpose(1, 0, 2)


def solution(mesh):
    return jax.shard_map(
        on_device,
        mesh=mesh,
        in_specs=(
            P("samp", "snp"),
            P("samp"),
            P("samp"),
            P("samp", None),
            P("snp", None, None),
            P("snp", None),
            P("snp"),
            P("snp"),
        ),
        out_specs=P("snp", None, None),
        check_vma=False,
    )
```

time: 24.3 us -> 28.7 us (1.18)
  Pallas kernels: 23.9 us -> 28.5 us
    pallas_call x1, Pallas kernels: 20.6 us -> 26.7 us  [reduced_sums(): pl.pallas_call(functools.partial(sums_kernel, count, ring, window), out_s...]
    pallas_call x1, Pallas kernels: 3.31 us -> 1.77 us  [on_device(): pl.pallas_call(functools.partial(scores_kernel, genotype.shape[0] * lax.a...]
where the time goes in v1:
time: 28.7 us; the launch traced here: 28.5 us
  Pallas kernels  28.5 us (99%)
    pallas_call x1, Pallas kernels, reduced_sums(): pl.pallas_call(functools.partial(sums_kernel, count, ring, window), out_s...  26.7 us
    pallas_call x1, Pallas kernels, on_device(): pl.pallas_call(functools.partial(scores_kernel, genotype.shape[0] * lax.a...  1.77 us

profile of v1, /device:TPU:0, one launch (start us, length us, event | category | flops | bytes accessed | tf_op | source)
XLA Modules:
  0.0 28.5 jit_solution(7981857970619633637)
XLA Ops:
  0.0 26.7 %sums.1 = (bf16[2,8,32,128]{3,2,1,0:T(8,128)(2,1)S(1)}, bf16[8,32,128]{2,1,0:T(8,128)(2,1)S(1)}, bf16[8,16,128]{2,1,0:T(8,128)(2,1)S(1)}, bf16[2,784,256]{2,1,0:T(8,128)(2,1)S(1)}) custom-call(bf16[2048,256]{1,0:T(8,128)(2,1)} %geno.1, f32[16,128]{1,0:T(8,128)} %bitcast.7, f32[16,128]{1,0:T(8,128)} %bitcast.8, s32[2048,127]{1,0:T(8,128)} %flips.1, ...), custom_call_target="tpu_custom_call" | custom-call | tf_op jit(solution)/shard_map/sums/pallas_call | solution.py:387
  26.7 1.8 %scores.1 = f32[49,32,128]{2,1,0:T(8,128)} custom-call(bf16[2,8,32,128]{3,2,1,0:T(8,128)(2,1)S(1)} %get-tuple-element.9.near, bf16[8,32,128]{2,1,0:T(8,128)(2,1)S(1)} %get-tuple-element.10.far, bf16[8,16,128]{2,1,0:T(8,128)(2,1)S(1)} %get-tuple-element.11.corner, bf16[2,784,256]{2,1,0:T(8,128)(2,1)S(1)} %get-tuple-element.12.placed), custom_call_target="tpu_custom_call" | custom-call | tf_op jit(solution)/shard_map/scores/pallas_call | solution.py:479

commit v2 on v1

v2 whole, which is shorter than its diff:
```python
import functools

import jax
import jax.numpy as jnp
from jax import lax
from jax.experimental import pallas as pl
from jax.experimental.pallas import tpu as pltpu
from jax.sharding import PartitionSpec as P

MESH = pl.DeviceIdType.MESH
TILE = 16
PARTS = 4
VMEM_LIMIT = 24 * 1024 * 1024


def across(left, right):
    return lax.dot_general(left, right, (((0,), (0,)), ((), ())), preferred_element_type=jnp.float32)


def iotas(rows, cols):
    return (
        lax.broadcasted_iota(jnp.int32, (rows, cols), 0),
        lax.broadcasted_iota(jnp.int32, (rows, cols), 1),
    )


def share_of(rows, count):
    per = -(-rows // (count * TILE)) * TILE
    while rows % per:
        per += TILE
    return per


def square_of(rows):
    tiles, width = rows.shape
    return jnp.concatenate([rows, jnp.zeros((width - tiles, width), jnp.float32)], axis=0)


def sums_kernel(
    count, ring, window,
    geno, phen, resid, flips, starts, ends, member, weights,
    near_out, far_out, corner_out, placed_out,
    phen_v, resid_v, starts_v, ends_v, member_v, weights_v,
    data_v, flips_v, halo_v,
    main_s, main_r, main_p, main_g,
    late_s, late_r, tail_v, tail_sums, sums_s, sums_r, sums_t, cols_v,
    load_sem, flip_sem, small_sem, halo_ss, halo_rs,
    ms_ss, ms_rs, mg_ss, mg_rs, lt_ss, lt_rs, td_ss, td_rs,
    sm_ss, sm_rs, tl_ss, tl_rs,
):
    me = lax.axis_index("samp")
    mine = lax.axis_index("snp")
    has_before = mine > 0
    has_after = mine < ring - 1
    odd = lax.rem(mine, 2) == 1
    even = lax.rem(mine, 2) == 0
    before = jnp.maximum(mine - 1, 0)
    after = jnp.minimum(mine + 1, ring - 1)
    samples = data_v.shape[0]
    owners, bands, per, _ = main_g.shape
    blocks = bands // 2
    snps = blocks * window
    part = samples // PARTS
    inverse = 1.0 / (samples * count)

    def peers(body, first=1):
        if count <= 16:
            for dist in range(first, count):
                body(dist)
        else:
            def step(dist, carry):
                body(dist)
                return carry
            lax.fori_loop(first, count, step, 0)

    def collect(wait, got, total):
        if count <= 16:
            for dist in range(1, count):
                wait(dist)
                total += got[dist].astype(jnp.float32)
            return total

        def step(dist, total):
            wait(dist)
            return total + got[dist].astype(jnp.float32)
        return lax.fori_loop(1, count, step, total)

    def ahead(dist):
        return lax.rem(me + dist, count)

    def behind(dist):
        return lax.rem(me + count - dist, count)

    barrier = pltpu.get_barrier_semaphore()

    def greet(dist, other):
        pl.semaphore_signal(barrier, inc=1, device_id=(ahead(dist), other), device_id_type=MESH)

    peers(lambda dist: greet(dist, mine))
    pl.when(has_before & even)(lambda: peers(lambda dist: greet(dist, before), 0))
    pl.when(has_before & odd)(lambda: greet(0, before))
    pl.when(has_after & odd)(lambda: peers(lambda dist: greet(dist, after), 0))
    pl.when(has_after & even)(lambda: greet(0, after))

    small = [
        pltpu.make_async_copy(src, dst, small_sem.at[i])
        for i, (src, dst) in enumerate((
            (resid, resid_v), (phen, phen_v), (starts, starts_v), (ends, ends_v),
            (member, member_v), (weights, weights_v),
        ))
    ]
    loads, flip_loads = [], []
    for copy in small[:2]:
        copy.start()
    for i in range(PARTS):
        rows = pl.ds(i * part, part)
        loads.append(pltpu.make_async_copy(
            geno.at[rows], data_v.at[rows, pl.ds(0, snps)], load_sem.at[i]))
        flip_loads.append(pltpu.make_async_copy(flips.at[rows], flips_v.at[rows], flip_sem.at[i]))
        flip_loads[i].start()
        loads[i].start()
    for copy in small[2:]:
        copy.start()

    for copy in small[:2]:
        copy.wait()
    phen_cols = square_of(phen_v[...]).T
    resid_cols = square_of(resid_v[...]).T
    lanes = phen_v.shape[1]
    for i in range(PARTS):
        flip_loads[i].wait()
        for t in range(i * part // lanes, (i + 1) * part // lanes):
            rows = pl.ds(t * lanes, lanes)
            signs = flips_v[rows, :].astype(jnp.float32)
            labels = jnp.concatenate([signs * resid_cols[:, t:t + 1], phen_cols[:, t:t + 1]], axis=1)
            data_v[rows, pl.ds(snps, window)] = labels.astype(jnp.bfloat16)

    from_before = jnp.where(has_before, jnp.where(even, count, 1), 0)
    from_after = jnp.where(has_after, jnp.where(even, 1, count), 0)
    pl.semaphore_wait(barrier, count - 1 + from_before + from_after)

    def remote(src, dst, ss, rs, device):
        return pltpu.make_async_remote_copy(
            src_ref=src, dst_ref=dst, send_sem=ss, recv_sem=rs,
            device_id=device, device_id_type=MESH)

    halos = []
    for i in range(PARTS):
        rows = pl.ds(i * part, part)
        halos.append(remote(
            geno.at[rows, pl.ds(0, window)], halo_v.at[rows],
            halo_ss.at[i], halo_rs.at[i], (me, before)))

    @pl.when(has_before)
    def _():
        for copy in halos:
            copy.start()

    def guarded(index, body):
        if owners == count:
            body()
        else:
            pl.when(index < owners)(body)

    def scatter_copy(dist):
        return remote(
            main_s.at[ahead(dist)], main_r.at[dist], ms_ss.at[dist], ms_rs.at[dist], (ahead(dist), mine))

    def gather_copy(dist, slot):
        return remote(main_p, main_g.at[slot], mg_ss.at[dist], mg_rs.at[dist], (ahead(dist), mine))

    def direct_copy(dist, slot):
        return remote(
            main_p.at[pl.ds(0, 2)], tail_v.at[slot], td_ss.at[dist], td_rs.at[dist], (ahead(dist), before))

    def sums_copy(dist):
        return remote(sums_s, sums_r.at[dist], sm_ss.at[dist], sm_rs.at[dist], (ahead(dist), mine))

    def late_copy(dist):
        return remote(late_s, late_r.at[dist], lt_ss.at[dist], lt_rs.at[dist], (ahead(dist), mine))

    tail_copies = [
        remote(sums_t, tail_sums, tl_ss.at[0], tl_rs.at[0], (me, before)),
        remote(main_g.at[:, pl.ds(0, 2)], tail_v, tl_ss.at[1], tl_rs.at[1], (me, before)),
    ]

    for i in range(PARTS):
        loads[i].wait()
    data = data_v[...]
    left = jnp.concatenate([data[:, :snps], jnp.ones((samples, 8), jnp.bfloat16)], axis=1)
    products = across(left, data)
    row8, _ = iotas(8, window)
    sums = jnp.zeros((8, window), jnp.float32)
    for b in range(blocks + 1):
        sums = jnp.where(row8 == b, products[snps:, b * window:(b + 1) * window], sums)
    sums_s[...] = sums
    peers(lambda dist: sums_copy(dist).start())
    row, col = iotas(window, window)
    for b in range(blocks):
        low, mid, high = b * window, (b + 1) * window, (b + 2) * window
        beyond = products[low:mid, mid:high] if b < blocks - 1 else 0.0
        band = jnp.where(col >= row, products[low:mid, low:mid], beyond)
        main_s[:, 2 * b] = products[low:mid, snps:].astype(jnp.bfloat16).reshape(owners, per, window)
        main_s[:, 2 * b + 1] = band.astype(jnp.bfloat16).reshape(owners, per, window)
    peers(lambda dist: guarded(ahead(dist), lambda: scatter_copy(dist).start()))

    half = window // 2
    half_row, half_col = iotas(half, window)

    def corner():
        for copy in halos:
            copy.wait_recv()
        product = across(data_v[:, pl.ds(snps - window, window)], halo_v[...])
        turned = pltpu.roll(product, half, 1)[:half]
        folded = jnp.where(half_col - half > half_row, product.T[half:], turned)
        late_s[...] = jnp.where(half_col < half, product[half:], folded).astype(jnp.bfloat16)
        peers(lambda dist: late_copy(dist).start())

    pl.when(has_after & even)(corner)

    for copy in small[2:]:
        copy.wait()
    place(mine * snps, starts_v, ends_v, member_v, weights_v, placed_out)

    sums_t[...] = collect(lambda dist: sums_copy(dist).wait_recv(), sums_r, sums_s[...])
    cols_v[...] = square_of(sums_t[...]).T
    pl.when(has_before)(lambda: tail_copies[0].start())

    def owner():
        total = collect(
            lambda dist: scatter_copy(dist).wait_recv(), main_r, main_s[me].astype(jnp.float32))
        row_of, col_of = iotas(per, window)
        row_of = row_of + me * per
        columns = cols_v[pl.ds(pl.multiple_of(me * per, per), per), :] * inverse
        for b in range(blocks):
            at = columns[:, b:b + 1]
            scored = total[2 * b] - at * sums_t[blocks:blocks + 1, :]
            main_p[2 * b] = pltpu.roll(scored, 1, 1).astype(main_p.dtype)
            mean_row = sums_t[b:b + 1, :] * inverse
            if b < blocks - 1:
                mean_row = jnp.where(col_of >= row_of, mean_row, sums_t[b + 1:b + 2, :] * inverse)
            value = total[2 * b + 1] * inverse - at * mean_row
            value = jnp.where(col_of == row_of, value, 2.0 * value)
            main_p[2 * b + 1] = value.astype(main_p.dtype)
        peers(lambda dist: gather_copy(dist, me).start())
        pl.when(has_before & even)(lambda: peers(lambda dist: direct_copy(dist, me).start(), 0))
        main_g[me] = main_p[...]
    guarded(me, owner)

    pl.when(has_after & odd)(corner)

    peers(lambda dist: guarded(
        behind(dist), lambda: gather_copy(dist, behind(dist)).wait_recv()))
    pl.when(has_before & odd)(lambda: tail_copies[1].start())
    near_out[...] = main_g[...]

    @pl.when(has_after)
    def _():
        folded = collect(
            lambda dist: late_copy(dist).wait_recv(), late_r, late_s[...].astype(jnp.float32))
        tail_copies[0].wait_recv()
        mirrored = jnp.concatenate([folded, folded], axis=0).T
        product = jnp.concatenate([
            pltpu.roll(folded, half, 1), jnp.where(half_col < half, folded, mirrored[half:])], axis=0)
        value = product * inverse - (cols_v[:, blocks - 1:blocks] * inverse) * (tail_sums[0:1, :] * inverse)
        corner_out[...] = jnp.where(col < row, 2.0 * value, 0.0).astype(corner_out.dtype)

        pl.when(even)(lambda: tail_copies[1].wait_recv())
        pl.when(odd)(lambda: peers(lambda dist: guarded(
            behind(dist), lambda: direct_copy(dist, behind(dist)).wait_recv()), 0))
        far_out[...] = tail_v[...]

    @pl.when(jnp.logical_not(has_after))
    def _():
        corner_out[...] = jnp.zeros_like(corner_out)
        far_out[...] = jnp.zeros_like(far_out)

    @pl.when(has_before)
    def _():
        for copy in halos:
            copy.wait_send()
        tail_copies[0].wait_send()
        pl.when(odd)(lambda: tail_copies[1].wait_send())
        pl.when(even)(lambda: guarded(
            me, lambda: peers(lambda dist: direct_copy(dist, me).wait_send(), 0)))
    peers(lambda dist: sums_copy(dist).wait_send())
    peers(lambda dist: guarded(ahead(dist), lambda: scatter_copy(dist).wait_send()))
    guarded(me, lambda: peers(lambda dist: gather_copy(dist, me).wait_send()))
    pl.when(has_after)(lambda: peers(lambda dist: late_copy(dist).wait_send()))


def place(offset, starts, ends, member, weights, placed):
    tissues, genes, window = weights.shape
    blocks = placed.shape[0]
    per_block = genes // blocks
    gene_row, gene_col = iotas(genes, genes)

    def upright(row_ref):
        spread = jnp.broadcast_to(row_ref[...].astype(jnp.float32), (genes, genes))
        picked = jnp.where(gene_row == gene_col, spread, 0.0)
        return jnp.sum(picked, axis=1, keepdims=True).astype(jnp.int32)

    first, past = upright(starts), upright(ends)
    gene, lane = iotas(genes, window)
    inside = lane < past - first
    within = first - offset - (gene // per_block) * window
    owned = member[...]
    for t in range(tissues):
        kept = inside & (owned[:, t:t + 1] != 0)
        weights[t] = jnp.where(kept, weights[t].astype(jnp.float32), 0.0).astype(weights.dtype)
    near = lane >= within
    source = (lane - within) & (window - 1)
    for t in range(tissues):
        turned = jnp.take_along_axis(weights[t].astype(jnp.float32), source, axis=1)
        head = jnp.where(near, turned, 0.0).astype(placed.dtype)
        rest = jnp.where(near, 0.0, turned).astype(placed.dtype)
        rows = pl.ds(t * per_block, per_block)
        for b in range(blocks):
            genes_of = slice(b * per_block, (b + 1) * per_block)
            placed[b, rows, pl.ds(0, window)] = head[genes_of]
            placed[b, rows, pl.ds(window, window)] = rest[genes_of]


def reduced_sums(genotype, phenotype, residual, sign_flips, starts, ends, member, weights):
    samples, snps = genotype.shape
    tissues, genes, window = weights.shape
    count, ring = lax.axis_size("samp"), lax.axis_size("snp")
    blocks = snps // window
    per = share_of(window, count)
    owners = window // per
    half, wide = jnp.bfloat16, jnp.float32
    dma = pltpu.SemaphoreType.DMA
    vmem = pl.BlockSpec(memory_space=pltpu.VMEM)
    hbm = pl.BlockSpec(memory_space=pltpu.HBM)
    operands = (
        genotype, phenotype.reshape(-1, window), residual.reshape(-1, window), sign_flips,
        starts.reshape(1, genes), ends.reshape(1, genes), member, weights,
    )
    return pl.pallas_call(
        functools.partial(sums_kernel, count, ring, window),
        out_shape=(
            jax.ShapeDtypeStruct((owners, 2 * blocks, per, window), half),
            jax.ShapeDtypeStruct((owners, 2, per, window), half),
            jax.ShapeDtypeStruct((window, window), half),
            jax.ShapeDtypeStruct((blocks, tissues * genes // blocks, 2 * window), half),
        ),
        in_specs=[hbm] * 8,
        out_specs=(vmem,) * 4,
        scratch_shapes=[pltpu.VMEM(x.shape, x.dtype) for x in operands[1:3] + operands[4:]] + [
            pltpu.VMEM((samples, snps + window), half),
            pltpu.VMEM(sign_flips.shape, jnp.int32),
            pltpu.VMEM((samples, window), half),
            pltpu.VMEM((owners, 2 * blocks, per, window), half),
            pltpu.VMEM((count, 2 * blocks, per, window), half),
            pltpu.VMEM((2 * blocks, per, window), half),
            pltpu.VMEM((owners, 2 * blocks, per, window), half),
            pltpu.VMEM((window // 2, window), half),
            pltpu.VMEM((count, window // 2, window), half),
            pltpu.VMEM((owners, 2, per, window), half),
            pltpu.VMEM((8, window), wide),
            pltpu.VMEM((8, window), wide),
            pltpu.VMEM((count, 8, window), wide),
            pltpu.VMEM((8, window), wide),
            pltpu.VMEM((window, window), wide),
            dma((PARTS,)), dma((PARTS,)), dma((6,)), dma((PARTS,)), dma((PARTS,)),
            dma((count,)), dma((count,)), dma((count,)), dma((count,)),
            dma((count,)), dma((count,)), dma((count,)), dma((count,)),
            dma((count,)), dma((count,)), dma((2,)), dma((2,)),
        ],
        compiler_params=pltpu.CompilerParams(
            collective_id=0, has_side_effects=True, vmem_limit_bytes=VMEM_LIMIT),
        name="sums",
    )(*(pltpu.with_memory_space_constraint(x, pltpu.HBM) for x in operands))


def scores_kernel(sample_total, near, far, corner, placed, out_hbm, out, sem):
    tissues, genes, window = out.shape
    blocks = placed.shape[0]
    per_block = genes // blocks
    row, col = iotas(window, window)
    root = 1.0 / (sample_total ** 0.5)

    def piece(b, kind):
        ref, at = (near, 2 * b) if b < blocks else (far, 0)
        return ref[:, at + kind].reshape(window, window)

    def masked(keep, value):
        return jnp.where(keep, value.astype(jnp.float32), 0.0).astype(jnp.bfloat16)

    labelled = [piece(b, 0) for b in range(blocks + 1)]
    banded = [piece(b, 1) for b in range(blocks + 1)]
    diagonal = [masked(col >= row, band) for band in banded]
    beside = [masked(col < row, band) for band in banded[:blocks - 1]] + [corner[...]]
    nothing = jnp.zeros((window, window), jnp.bfloat16)
    pairs, bands = [], []
    for b in range(blocks):
        pairs.append(jnp.concatenate([labelled[b], labelled[b + 1]], axis=0))
        bands.append(jnp.concatenate([
            jnp.concatenate([diagonal[b], beside[b]], axis=1),
            jnp.concatenate([nothing, diagonal[b + 1]], axis=1),
        ], axis=0))

    copies = []
    step = next(n for n in range(min(7, tissues), 0, -1) if tissues % n == 0)
    for t in range(0, tissues, step):
        for b in range(blocks):
            half = placed[b, pl.ds(t * per_block, step * per_block), :]
            top = jnp.dot(half, pairs[b], preferred_element_type=jnp.float32)
            square = jnp.dot(half, bands[b], preferred_element_type=jnp.float32)
            variance = jnp.sum(square * half.astype(jnp.float32), axis=1, keepdims=True)
            scale = lax.rsqrt(jnp.maximum(variance, 0.0) + 1e-06) * root
            out[pl.ds(t, step), pl.ds(b * per_block, per_block), :] = (top * scale).reshape(step, per_block, window)
        part = pl.ds(t, step)
        copies.append(pltpu.make_async_copy(out.at[part], out_hbm.at[part], sem.at[t // step]))
        copies[-1].start()
    for copy in copies:
        copy.wait()


def on_device(genotype, phenotype, residual, sign_flips, weights, member, gene_start, gene_end):
    by_tissue = weights.transpose(1, 0, 2)
    near, far, corner, placed = reduced_sums(
        genotype, phenotype, residual, sign_flips, gene_start, gene_end, member, by_tissue)
    vmem = pl.BlockSpec(memory_space=pltpu.VMEM)
    scores = pl.pallas_call(
        functools.partial(scores_kernel, genotype.shape[0] * lax.axis_size("samp")),
        out_shape=jax.ShapeDtypeStruct(by_tissue.shape, jnp.float32),
        in_specs=[vmem] * 4,
        out_specs=pl.BlockSpec(memory_space=pltpu.HBM),
        scratch_shapes=[
            pltpu.VMEM(by_tissue.shape, jnp.float32),
            pltpu.SemaphoreType.DMA((by_tissue.shape[0],)),
        ],
        compiler_params=pltpu.CompilerParams(vmem_limit_bytes=VMEM_LIMIT),
        name="scores",
    )(near, far, corner, placed)
    return scores.transpose(1, 0, 2)


def solution(mesh):
    return jax.shard_map(
        on_device,
        mesh=mesh,
        in_specs=(
            P("samp", "snp"),
            P("samp"),
            P("samp"),
            P("samp", None),
            P("snp", None, None),
            P("snp", None),
            P("snp"),
            P("snp"),
        ),
        out_specs=P("snp", None, None),
        check_vma=False,
    )
```

time: 28.7 us -> 21.4 us (0.75)
  the two profiles are of different devices: /device:TPU:0 before, /device:TPU:1 now
where the time goes in v2:
time: 21.4 us; the launch traced here: 21.2 us
  Pallas kernels  21.2 us (99%)
    pallas_call x1, Pallas kernels, reduced_sums(): pl.pallas_call(functools.partial(sums_kernel, count, ring, window), out_s...  19.4 us
    pallas_call x1, Pallas kernels, on_device(): pl.pallas_call(functools.partial(scores_kernel, genotype.shape[0] * lax.a...  1.77 us

profile of v2, /device:TPU:1, one launch (start us, length us, event | category | flops | bytes accessed | tf_op | source)
XLA Modules:
  0.0 21.2 jit_solution(12773291943605997797)
XLA Ops:
  0.0 19.4 %sums.1 = (bf16[8,4,16,128]{3,2,1,0:T(8,128)(2,1)S(1)}, bf16[8,2,16,128]{3,2,1,0:T(8,128)(2,1)S(1)}, bf16[128,128]{1,0:T(8,128)(2,1)S(1)}, bf16[2,784,256]{2,1,0:T(8,128)(2,1)S(1)}) custom-call(bf16[2048,256]{1,0:T(8,128)(2,1)} %geno.1, f32[16,128]{1,0:T(8,128)} %bitcast.7, f32[16,128]{1,0:T(8,128)} %bitcast.8, s32[2048,127]{1,0:T(8,128)} %flips.1, ...), custom_call_target="tpu_custom_call" | custom-call | tf_op jit(solution)/shard_map/sums/pallas_call | solution.py:339
  19.4 1.8 %scores.1 = f32[49,32,128]{2,1,0:T(8,128)} custom-call(bf16[8,4,16,128]{3,2,1,0:T(8,128)(2,1)S(1)} %get-tuple-element.9.near, bf16[8,2,16,128]{3,2,1,0:T(8,128)(2,1)S(1)} %get-tuple-element.10.far, bf16[128,128]{1,0:T(8,128)(2,1)S(1)} %get-tuple-element.11.corner, bf16[2,784,256]{2,1,0:T(8,128)(2,1)S(1)} %get-tuple-element.12.placed), custom_call_target="tpu_custom_call" | custom-call | tf_op jit(solution)/shard_map/scores/pallas_call | solution.py:425

commit v3 on v2

--- a/solution.py
+++ b/solution.py
@@ -41,12 +41,12 @@
     geno, phen, resid, flips, starts, ends, member, weights,
     near_out, far_out, corner_out, placed_out,
     phen_v, resid_v, starts_v, ends_v, member_v, weights_v,
-    data_v, flips_v, halo_v,
+    data_v, flips_v, halo_v, back_v,
     main_s, main_r, main_p, main_g,
-    late_s, late_r, tail_v, tail_sums, sums_s, sums_r, sums_t, cols_v,
+    late_s, late_r, back_s, back_r, fold_v, tail_v, tail_sums, sums_s, sums_r, sums_t, cols_v,
     load_sem, flip_sem, small_sem, halo_ss, halo_rs,
-    ms_ss, ms_rs, mg_ss, mg_rs, lt_ss, lt_rs, td_ss, td_rs,
-    sm_ss, sm_rs, tl_ss, tl_rs,
+    ms_ss, ms_rs, mg_ss, mg_rs, lt_ss, lt_rs, bc_ss, bc_rs, td_ss, td_rs,
+    sm_ss, sm_rs, tl_ss, tl_rs, bk_ss, bk_rs,
 ):
     me = lax.axis_index("samp")
     mine = lax.axis_index("snp")
@@ -151,10 +151,23 @@
             geno.at[rows, pl.ds(0, window)], halo_v.at[rows],
             halo_ss.at[i], halo_rs.at[i], (me, before)))
 
+    half_parts = PARTS // 2
+    split = half_parts * part
+    back = remote(
+        geno.at[pl.ds(split, samples - split), pl.ds(snps - window, window)], back_v,
+        bk_ss.at[0], bk_rs.at[0], (me, after))
+
     @pl.when(has_before)
     def _():
-        for copy in halos:
+        for copy in halos[:half_parts]:
             copy.start()
+
+    @pl.when(has_before & odd)
+    def _():
+        for copy in halos[half_parts:]:
+            copy.start()
+
+    pl.when(has_after & odd)(back.start)
 
     def guarded(index, body):
         if owners == count:
@@ -178,6 +191,9 @@
 
     def late_copy(dist):
         return remote(late_s, late_r.at[dist], lt_ss.at[dist], lt_rs.at[dist], (ahead(dist), mine))
+
+    def back_copy(dist):
+        return remote(back_s, back_r.at[dist], bc_ss.at[dist], bc_rs.at[dist], (ahead(dist), before))
 
     tail_copies = [
         remote(sums_t, tail_sums, tl_ss.at[0], tl_rs.at[0], (me, before)),
@@ -207,20 +223,29 @@
     half = window // 2
     half_row, half_col = iotas(half, window)
 
-    def corner():
-        for copy in halos:
-            copy.wait_recv()
-        product = across(data_v[:, pl.ds(snps - window, window)], halo_v[...])
+    def fold(product):
         turned = pltpu.roll(product, half, 1)[:half]
         folded = jnp.where(half_col - half > half_row, product.T[half:], turned)
-        late_s[...] = jnp.where(half_col < half, product[half:], folded).astype(jnp.bfloat16)
+        return jnp.where(half_col < half, product[half:], folded).astype(jnp.bfloat16)
+
+    def corner(count_of_parts):
+        for copy in halos[:count_of_parts]:
+            copy.wait_recv()
+        rows = pl.ds(0, count_of_parts * part)
+        late_s[...] = fold(across(data_v[rows, pl.ds(snps - window, window)], halo_v[rows, :]))
         peers(lambda dist: late_copy(dist).start())
 
-    pl.when(has_after & even)(corner)
+    pl.when(has_after & even)(lambda: corner(PARTS))
 
     for copy in small[2:]:
         copy.wait()
     place(mine * snps, starts_v, ends_v, member_v, weights_v, placed_out)
+
+    @pl.when(has_before & even)
+    def _():
+        back.wait_recv()
+        back_s[...] = fold(across(back_v[...], data_v[pl.ds(split, samples - split), pl.ds(0, window)]))
+        peers(lambda dist: back_copy(dist).start(), 0)
 
     sums_t[...] = collect(lambda dist: sums_copy(dist).wait_recv(), sums_r, sums_s[...])
     cols_v[...] = square_of(sums_t[...]).T
@@ -247,7 +272,7 @@
         main_g[me] = main_p[...]
     guarded(me, owner)
 
-    pl.when(has_after & odd)(corner)
+    pl.when(has_after & odd)(lambda: corner(half_parts))
 
     peers(lambda dist: guarded(
         behind(dist), lambda: gather_copy(dist, behind(dist)).wait_recv()))
@@ -256,8 +281,16 @@
 
     @pl.when(has_after)
     def _():
-        folded = collect(
+        fold_v[...] = collect(
             lambda dist: late_copy(dist).wait_recv(), late_r, late_s[...].astype(jnp.float32))
+
+        @pl.when(odd)
+        def _():
+            back_copy(0).wait_recv()
+            fold_v[...] += collect(
+                lambda dist: back_copy(dist).wait_recv(), back_r, back_r[0].astype(jnp.float32))
+
+        folded = fold_v[...]
         tail_copies[0].wait_recv()
         mirrored = jnp.concatenate([folded, folded], axis=0).T
         product = jnp.concatenate([
@@ -277,12 +310,20 @@
 
     @pl.when(has_before)
     def _():
-        for copy in halos:
+        for copy in halos[:half_parts]:
             copy.wait_send()
         tail_copies[0].wait_send()
-        pl.when(odd)(lambda: tail_copies[1].wait_send())
+
+        @pl.when(odd)
+        def _():
+            for copy in halos[half_parts:]:
+                copy.wait_send()
+            tail_copies[1].wait_send()
+
+        pl.when(even)(lambda: peers(lambda dist: back_copy(dist).wait_send(), 0))
         pl.when(even)(lambda: guarded(
             me, lambda: peers(lambda dist: direct_copy(dist, me).wait_send(), 0)))
+    pl.when(has_after & odd)(back.wait_send)
     peers(lambda dist: sums_copy(dist).wait_send())
     peers(lambda dist: guarded(ahead(dist), lambda: scatter_copy(dist).wait_send()))
     guarded(me, lambda: peers(lambda dist: gather_copy(dist, me).wait_send()))
@@ -350,12 +391,16 @@
             pltpu.VMEM((samples, snps + window), half),
             pltpu.VMEM(sign_flips.shape, jnp.int32),
             pltpu.VMEM((samples, window), half),
+            pltpu.VMEM((samples - samples // PARTS * (PARTS // 2), window), half),
             pltpu.VMEM((owners, 2 * blocks, per, window), half),
             pltpu.VMEM((count, 2 * blocks, per, window), half),
             pltpu.VMEM((2 * blocks, per, window), half),
             pltpu.VMEM((owners, 2 * blocks, per, window), half),
             pltpu.VMEM((window // 2, window), half),
             pltpu.VMEM((count, window // 2, window), half),
+            pltpu.VMEM((window // 2, window), half),
+            pltpu.VMEM((count, window // 2, window), half),
+            pltpu.VMEM((window // 2, window), wide),
             pltpu.VMEM((owners, 2, per, window), half),
             pltpu.VMEM((8, window), wide),
             pltpu.VMEM((8, window), wide),
@@ -365,7 +410,8 @@
             dma((PARTS,)), dma((PARTS,)), dma((6,)), dma((PARTS,)), dma((PARTS,)),
             dma((count,)), dma((count,)), dma((count,)), dma((count,)),
             dma((count,)), dma((count,)), dma((count,)), dma((count,)),
-            dma((count,)), dma((count,)), dma((2,)), dma((2,)),
+            dma((count,)), dma((count,)), dma((count,)), dma((count,)),
+            dma((2,)), dma((2,)), dma((1,)), dma((1,)),
         ],
         compiler_params=pltpu.CompilerParams(
             collective_id=0, has_side_effects=True, vmem_limit_bytes=VMEM_LIMIT),

time: 21.4 us -> 21.6 us (level)
    pallas_call x1, Pallas kernels: 19.4 us -> 19.7 us  [reduced_sums(): pl.pallas_call(functools.partial(sums_kernel, count, ring, window), out_s...]
where the time goes in v3:
time: 21.6 us; the launch traced here: 21.4 us
  Pallas kernels  21.4 us (99%)
    pallas_call x1, Pallas kernels, reduced_sums(): pl.pallas_call(functools.partial(sums_kernel, count, ring, window), out_s...  19.7 us
    pallas_call x1, Pallas kernels, on_device(): pl.pallas_call(functools.partial(scores_kernel, genotype.shape[0] * lax.a...  1.77 us

profile of v3, /device:TPU:1, one launch (start us, length us, event | category | flops | bytes accessed | tf_op | source)
XLA Modules:
  0.0 21.4 jit_solution(5395399195191319128)
XLA Ops:
  0.0 19.7 %sums.1 = (bf16[8,4,16,128]{3,2,1,0:T(8,128)(2,1)S(1)}, bf16[8,2,16,128]{3,2,1,0:T(8,128)(2,1)S(1)}, bf16[128,128]{1,0:T(8,128)(2,1)S(1)}, bf16[2,784,256]{2,1,0:T(8,128)(2,1)S(1)}) custom-call(bf16[2048,256]{1,0:T(8,128)(2,1)} %geno.1, f32[16,128]{1,0:T(8,128)} %bitcast.7, f32[16,128]{1,0:T(8,128)} %bitcast.8, s32[2048,127]{1,0:T(8,128)} %flips.1, ...), custom_call_target="tpu_custom_call" | custom-call | tf_op jit(solution)/shard_map/sums/pallas_call | solution.py:380
  19.7 1.8 %scores.1 = f32[49,32,128]{2,1,0:T(8,128)} custom-call(bf16[8,4,16,128]{3,2,1,0:T(8,128)(2,1)S(1)} %get-tuple-element.9.near, bf16[8,2,16,128]{3,2,1,0:T(8,128)(2,1)S(1)} %get-tuple-element.10.far, bf16[128,128]{1,0:T(8,128)(2,1)S(1)} %get-tuple-element.11.corner, bf16[2,784,256]{2,1,0:T(8,128)(2,1)S(1)} %get-tuple-element.12.placed), custom_call_target="tpu_custom_call" | custom-call | tf_op jit(solution)/shard_map/scores/pallas_call | solution.py:471

commit v4 on v3

v4 whole, which is shorter than its diff:
```python
import functools

import jax
import jax.numpy as jnp
from jax import lax
from jax.experimental import pallas as pl
from jax.experimental.pallas import tpu as pltpu
from jax.sharding import PartitionSpec as P

MESH = pl.DeviceIdType.MESH
TILE = 16
PARTS = 4
HALVES = 2
VMEM_LIMIT = 24 * 1024 * 1024


def across(left, right):
    return lax.dot_general(left, right, (((0,), (0,)), ((), ())), preferred_element_type=jnp.float32)


def iotas(rows, cols):
    return (
        lax.broadcasted_iota(jnp.int32, (rows, cols), 0),
        lax.broadcasted_iota(jnp.int32, (rows, cols), 1),
    )


def share_of(rows, count):
    per = -(-rows // (count * TILE)) * TILE
    while rows % per:
        per += TILE
    return per


def square_of(rows):
    tiles, width = rows.shape
    return jnp.concatenate([rows, jnp.zeros((width - tiles, width), jnp.float32)], axis=0)


def sums_kernel(
    count, ring, window,
    geno, phen, resid, flips, starts, ends, member, weights,
    near_out, far_out, corner_out, placed_out,
    phen_v, resid_v, starts_v, ends_v, member_v, weights_v,
    data_v, flips_v, halo_v, back_v,
    main_s, main_r, main_p, main_g,
    late_s, late_r, back_s, back_r, fold_v, tail_v,
    sums_s, sums_r, sums_t, cols_v, near_v, next_v,
    load_sem, flip_sem, small_sem, halo_ss, halo_rs,
    ms_ss, ms_rs, mg_ss, mg_rs, lt_ss, lt_rs, bc_ss, bc_rs, td_ss, td_rs,
    sm_ss, sm_rs, st_ss, st_rs, bk_ss, bk_rs,
):
    me = lax.axis_index("samp")
    mine = lax.axis_index("snp")
    parity = lax.rem(mine, 2)
    odd, even = parity == 1, parity == 0
    has_before, has_after = mine > 0, mine < ring - 1
    before = jnp.maximum(mine - 1, 0)
    after = jnp.minimum(mine + 1, ring - 1)
    beyond = jnp.minimum(mine + 2, ring - 1)
    keeper = mine + 1 - parity
    partner = mine + 1 - 2 * parity
    slot = 1 - parity
    samples = data_v.shape[0]
    owners, bands, per, _ = main_g.shape
    blocks = bands // 2
    snps = blocks * window
    part = samples // PARTS
    split = samples // HALVES
    inverse = 1.0 / (samples * count)

    def peers(body, first=1):
        if count <= 16:
            for dist in range(first, count):
                body(dist)
        else:
            def step(dist, carry):
                body(dist)
                return carry
            lax.fori_loop(first, count, step, 0)

    def group(body):
        pl.when(even)(lambda: body(0))
        peers(body)

    def collect(wait, got, total, first=1):
        if count <= 16:
            for dist in range(first, count):
                wait(dist)
                total += got[dist].astype(jnp.float32)
            return total

        def step(dist, total):
            wait(dist)
            return total + got[dist].astype(jnp.float32)
        return lax.fori_loop(first, count, step, total)

    def ahead(dist):
        return lax.rem(me + dist, count)

    def behind(dist):
        return lax.rem(me + count - dist, count)

    small = [
        pltpu.make_async_copy(src, dst, small_sem.at[i])
        for i, (src, dst) in enumerate((
            (resid, resid_v), (phen, phen_v), (starts, starts_v), (ends, ends_v),
            (member, member_v), (weights, weights_v),
        ))
    ]
    flip_loads = []
    for copy in small[:2]:
        copy.start()
    for i in range(PARTS):
        rows = pl.ds(i * part, part)
        flip_loads.append(pltpu.make_async_copy(flips.at[rows], flips_v.at[rows], flip_sem.at[i]))
        flip_loads[i].start()
    load = pltpu.make_async_copy(geno, data_v.at[:, pl.ds(0, snps)], load_sem.at[0])
    load.start()

    barrier = pltpu.get_barrier_semaphore()

    def greet(dist, other):
        pl.semaphore_signal(barrier, inc=1, device_id=(ahead(dist), other), device_id_type=MESH)

    peers(lambda dist: greet(dist, mine))
    peers(lambda dist: greet(dist, partner), 0)
    pl.when(has_before & even)(lambda: greet(0, before))

    @pl.when(has_after & odd)
    def _():
        peers(lambda dist: greet(dist, after), 0)
        peers(lambda dist: greet(dist, beyond), 0)

    for copy in small[2:]:
        copy.start()

    for copy in small[:2]:
        copy.wait()
    phen_cols = square_of(phen_v[...]).T
    resid_cols = square_of(resid_v[...]).T
    lanes = phen_v.shape[1]
    for i in range(PARTS):
        flip_loads[i].wait()
        for t in range(i * part // lanes, (i + 1) * part // lanes):
            rows = pl.ds(t * lanes, lanes)
            signs = flips_v[rows, :].astype(jnp.float32)
            labels = jnp.concatenate([signs * resid_cols[:, t:t + 1], phen_cols[:, t:t + 1]], axis=1)
            data_v[rows, pl.ds(snps, window)] = labels.astype(jnp.bfloat16)

    load.wait()
    data = data_v[...]
    left = jnp.concatenate([data[:, :snps], jnp.ones((samples, 8), jnp.bfloat16)], axis=1)
    products = across(left, data)
    row8, _ = iotas(8, window)
    sums = jnp.zeros((8, window), jnp.float32)
    for b in range(blocks + 1):
        sums = jnp.where(row8 == b, products[snps:, b * window:(b + 1) * window], sums)
    sums_s[...] = sums
    row, col = iotas(window, window)
    for b in range(blocks):
        low, mid, high = b * window, (b + 1) * window, (b + 2) * window
        other = products[low:mid, mid:high] if b < blocks - 1 else 0.0
        band = jnp.where(col >= row, products[low:mid, low:mid], other)
        main_s[:, 2 * b] = products[low:mid, snps:].astype(jnp.bfloat16).reshape(owners, per, window)
        main_s[:, 2 * b + 1] = band.astype(jnp.bfloat16).reshape(owners, per, window)

    def remote(src, dst, ss, rs, device):
        return pltpu.make_async_remote_copy(
            src_ref=src, dst_ref=dst, send_sem=ss, recv_sem=rs,
            device_id=device, device_id_type=MESH)

    halos = []
    for i in range(HALVES):
        rows = pl.ds(i * split, split)
        halos.append(remote(
            geno.at[rows, pl.ds(0, window)], halo_v.at[rows],
            halo_ss.at[i], halo_rs.at[i], (me, before)))
    back = remote(
        geno.at[pl.ds(split, samples - split), pl.ds(snps - window, window)], back_v,
        bk_ss.at[0], bk_rs.at[0], (me, after))

    def guarded(index, body):
        if owners == count:
            body()
        else:
            pl.when(index < owners)(body)

    def sums_copy(dist):
        return remote(
            sums_s, sums_r.at[slot, dist], sm_ss.at[dist], sm_rs.at[slot, dist], (ahead(dist), keeper))

    def scatter_copy(dist):
        return remote(
            main_s.at[ahead(dist)], main_r.at[slot, dist],
            ms_ss.at[dist], ms_rs.at[slot, dist], (ahead(dist), keeper))

    def gather_copy(s, dist, place):
        return remote(
            main_p.at[s], main_g.at[place], mg_ss.at[s, dist], mg_rs.at[dist],
            (ahead(dist), jnp.maximum(mine - s, 0)))

    def direct_copy(s, dist, place):
        return remote(
            main_p.at[s, pl.ds(0, 2)], tail_v.at[place], td_ss.at[s, dist], td_rs.at[dist],
            (ahead(dist), jnp.maximum(mine - 1 - s, 0)))

    def late_copy(dist):
        return remote(late_s, late_r.at[dist], lt_ss.at[dist], lt_rs.at[dist], (ahead(dist), mine))

    def back_copy(dist):
        return remote(back_s, back_r.at[dist], bc_ss.at[dist], bc_rs.at[dist], (ahead(dist), before))

    stats = [
        remote(sums_t.at[1], near_v, st_ss.at[0], st_rs.at[0], (me, before)),
        remote(sums_t.at[0], next_v, st_ss.at[1], st_rs.at[1], (me, before)),
        remote(sums_t.at[1], next_v, st_ss.at[2], st_rs.at[2], (me, jnp.maximum(mine - 2, 0))),
    ]
    further = odd & (mine > 1)

    pl.semaphore_wait(
        barrier,
        2 * count - 1 + jnp.where(has_before & even, count, 0)
        + jnp.where(has_after & odd, 1, 0) + jnp.where(further, count, 0))
    pl.when(has_before)(halos[0].start)

    @pl.when(has_before & odd)
    def _():
        for copy in halos[1:]:
            copy.start()

    pl.when(has_after & odd)(back.start)
    group(lambda dist: sums_copy(dist).start())
    group(lambda dist: guarded(ahead(dist), lambda: scatter_copy(dist).start()))

    half = window // 2
    half_row, half_col = iotas(half, window)

    def fold(product):
        turned = pltpu.roll(product, half, 1)[:half]
        folded = jnp.where(half_col - half > half_row, product.T[half:], turned)
        return jnp.where(half_col < half, product[half:], folded).astype(jnp.bfloat16)

    def corner(arrived):
        for copy in halos[:arrived]:
            copy.wait_recv()
        rows = pl.ds(0, arrived * split)
        late_s[...] = fold(across(data_v[rows, pl.ds(snps - window, window)], halo_v[rows, :]))
        peers(lambda dist: late_copy(dist).start())

    pl.when(even)(lambda: corner(HALVES))

    for copy in small[2:]:
        copy.wait()
    place(mine * snps, starts_v, ends_v, member_v, weights_v, placed_out)

    @pl.when(has_before & even)
    def _():
        back.wait_recv()
        back_s[...] = fold(across(back_v[...], data_v[pl.ds(split, samples - split), pl.ds(0, window)]))
        peers(lambda dist: back_copy(dist).start(), 0)

    def settle(s):
        sums_t[s] = collect(
            lambda dist: remote(
                sums_s, sums_r.at[s, dist], sm_ss.at[dist], sm_rs.at[s, dist],
                (ahead(dist), partner)).wait_recv(),
            sums_r.at[s], sums_s[...] if s == 0 else jnp.zeros_like(sums_s), 1 - s)
        cols_v[s] = square_of(sums_t[s]).T

    def own(s):
        def body():
            total = collect(
                lambda dist: remote(
                    main_s.at[0], main_r.at[s, dist], ms_ss.at[dist], ms_rs.at[s, dist],
                    (ahead(dist), partner)).wait_recv(),
                main_r.at[s],
                main_s[me].astype(jnp.float32) if s == 0 else jnp.zeros(main_p.shape[1:], jnp.float32), 1 - s)
            row_of, col_of = iotas(per, window)
            row_of = row_of + me * per
            columns = cols_v[s, pl.ds(pl.multiple_of(me * per, per), per), :] * inverse
            for b in range(blocks):
                at = columns[:, b:b + 1]
                scored = total[2 * b] - at * sums_t[s, blocks:blocks + 1, :]
                main_p[s, 2 * b] = pltpu.roll(scored, 1, 1).astype(main_p.dtype)
                mean_row = sums_t[s, b:b + 1, :] * inverse
                if b < blocks - 1:
                    mean_row = jnp.where(col_of >= row_of, mean_row, sums_t[s, b + 1:b + 2, :] * inverse)
                value = total[2 * b + 1] * inverse - at * mean_row
                value = jnp.where(col_of == row_of, value, 2.0 * value)
                main_p[s, 2 * b + 1] = value.astype(main_p.dtype)
            peers(lambda dist: gather_copy(s, dist, me).start(), 1 - s)
            if s == 0:
                peers(lambda dist: direct_copy(s, dist, me).start(), 0)
                main_g[me] = main_p[s]
            else:
                pl.when(further)(lambda: peers(lambda dist: direct_copy(s, dist, me).start(), 0))
        guarded(me, body)

    @pl.when(odd)
    def _():
        for s in range(2):
            settle(s)
        stats[0].start()
        stats[1].start()
        pl.when(further)(stats[2].start)
        for s in range(2):
            own(s)

    pl.when(has_after & odd)(lambda: corner(1))

    @pl.when(has_after)
    def _():
        @pl.when(even)
        def _():
            stats[0].wait_recv()
            stats[1].wait_recv()

        @pl.when(odd)
        def _():
            near_v[...] = sums_t[0]
            stats[2].wait_recv()

        fold_v[...] = collect(
            lambda dist: late_copy(dist).wait_recv(), late_r, late_s[...].astype(jnp.float32))

        @pl.when(odd)
        def _():
            fold_v[...] = collect(lambda dist: back_copy(dist).wait_recv(), back_r, fold_v[...], 0)

        folded = fold_v[...]
        mirrored = jnp.concatenate([folded, folded], axis=0).T
        product = jnp.concatenate([
            pltpu.roll(folded, half, 1), jnp.where(half_col < half, folded, mirrored[half:])], axis=0)
        mean_col = square_of(near_v[...]).T[:, blocks - 1:blocks] * inverse
        value = product * inverse - mean_col * (next_v[0:1, :] * inverse)
        corner_out[...] = jnp.where(col < row, 2.0 * value, 0.0).astype(corner_out.dtype)

    group(lambda dist: guarded(
        behind(dist), lambda: gather_copy(0, dist, behind(dist)).wait_recv()))
    near_out[...] = main_g[...]

    @pl.when(has_after)
    def _():
        peers(lambda dist: guarded(
            behind(dist), lambda: direct_copy(0, dist, behind(dist)).wait_recv()), 0)
        far_out[...] = tail_v[...]

    @pl.when(jnp.logical_not(has_after))
    def _():
        corner_out[...] = jnp.zeros_like(corner_out)
        far_out[...] = jnp.zeros_like(far_out)

    pl.when(has_before)(halos[0].wait_send)
    pl.when(has_before & even)(lambda: peers(lambda dist: back_copy(dist).wait_send(), 0))
    pl.when(has_after & odd)(back.wait_send)
    pl.when(has_after)(lambda: peers(lambda dist: late_copy(dist).wait_send()))
    group(lambda dist: sums_copy(dist).wait_send())
    group(lambda dist: guarded(ahead(dist), lambda: scatter_copy(dist).wait_send()))

    @pl.when(odd)
    def _():
        for copy in halos[1:]:
            copy.wait_send()
        stats[0].wait_send()
        stats[1].wait_send()
        pl.when(further)(stats[2].wait_send)

        def sent():
            for s in range(2):
                peers(lambda dist: gather_copy(s, dist, me).wait_send(), 1 - s)
            peers(lambda dist: direct_copy(0, dist, me).wait_send(), 0)
            pl.when(further)(lambda: peers(lambda dist: direct_copy(1, dist, me).wait_send(), 0))
        guarded(me, sent)


def place(offset, starts, ends, member, weights, placed):
    tissues, genes, window = weights.shape
    blocks = placed.shape[0]
    per_block = genes // blocks
    gene_row, gene_col = iotas(genes, genes)

    def upright(row_ref):
        spread = jnp.broadcast_to(row_ref[...].astype(jnp.float32), (genes, genes))
        picked = jnp.where(gene_row == gene_col, spread, 0.0)
        return jnp.sum(picked, axis=1, keepdims=True).astype(jnp.int32)

    first, past = upright(starts), upright(ends)
    gene, lane = iotas(genes, window)
    inside = lane < past - first
    within = first - offset - (gene // per_block) * window
    owned = member[...]
    for t in range(tissues):
        kept = inside & (owned[:, t:t + 1] != 0)
        weights[t] = jnp.where(kept, weights[t].astype(jnp.float32), 0.0).astype(weights.dtype)
    near = lane >= within
    source = (lane - within) & (window - 1)
    for t in range(tissues):
        turned = jnp.take_along_axis(weights[t].astype(jnp.float32), source, axis=1)
        head = jnp.where(near, turned, 0.0).astype(placed.dtype)
        rest = jnp.where(near, 0.0, turned).astype(placed.dtype)
        rows = pl.ds(t * per_block, per_block)
        for b in range(blocks):
            genes_of = slice(b * per_block, (b + 1) * per_block)
            placed[b, rows, pl.ds(0, window)] = head[genes_of]
            placed[b, rows, pl.ds(window, window)] = rest[genes_of]


def reduced_sums(genotype, phenotype, residual, sign_flips, starts, ends, member, weights):
    samples, snps = genotype.shape
    tissues, genes, window = weights.shape
    count, ring = lax.axis_size("samp"), lax.axis_size("snp")
    blocks = snps // window
    per = share_of(window, count)
    owners = window // per
    half, wide = jnp.bfloat16, jnp.float32
    dma = pltpu.SemaphoreType.DMA
    vmem = pl.BlockSpec(memory_space=pltpu.VMEM)
    hbm = pl.BlockSpec(memory_space=pltpu.HBM)
    operands = (
        genotype, phenotype.reshape(-1, window), residual.reshape(-1, window), sign_flips,
        starts.reshape(1, genes), ends.reshape(1, genes), member, weights,
    )
    return pl.pallas_call(
        functools.partial(sums_kernel, count, ring, window),
        out_shape=(
            jax.ShapeDtypeStruct((owners, 2 * blocks, per, window), half),
            jax.ShapeDtypeStruct((owners, 2, per, window), half),
            jax.ShapeDtypeStruct((window, window), half),
            jax.ShapeDtypeStruct((blocks, tissues * genes // blocks, 2 * window), half),
        ),
        in_specs=[hbm] * 8,
        out_specs=(vmem,) * 4,
        scratch_shapes=[pltpu.VMEM(x.shape, x.dtype) for x in operands[1:3] + operands[4:]] + [
            pltpu.VMEM((samples, snps + window), half),
            pltpu.VMEM(sign_flips.shape, jnp.int32),
            pltpu.VMEM((samples, window), half),
            pltpu.VMEM((samples - samples // HALVES, window), half),
            pltpu.VMEM((owners, 2 * blocks, per, window), half),
            pltpu.VMEM((2, count, 2 * blocks, per, window), half),
            pltpu.VMEM((2, 2 * blocks, per, window), half),
            pltpu.VMEM((owners, 2 * blocks, per, window), half),
            pltpu.VMEM((window // 2, window), half),
            pltpu.VMEM((count, window // 2, window), half),
            pltpu.VMEM((window // 2, window), half),
            pltpu.VMEM((count, window // 2, window), half),
            pltpu.VMEM((window // 2, window), wide),
            pltpu.VMEM((owners, 2, per, window), half),
            pltpu.VMEM((8, window), wide),
            pltpu.VMEM((2, count, 8, window), wide),
            pltpu.VMEM((2, 8, window), wide),
            pltpu.VMEM((2, window, window), wide),
            pltpu.VMEM((8, window), wide),
            pltpu.VMEM((8, window), wide),
            dma((1,)), dma((PARTS,)), dma((6,)), dma((HALVES,)), dma((HALVES,)),
            dma((count,)), dma((2, count)), dma((2, count)), dma((count,)),
            dma((count,)), dma((count,)), dma((count,)), dma((count,)), dma((2, count)), dma((count,)),
            dma((count,)), dma((2, count)), dma((3,)), dma((3,)), dma((1,)), dma((1,)),
        ],
        compiler_params=pltpu.CompilerParams(
            collective_id=0, has_side_effects=True, vmem_limit_bytes=VMEM_LIMIT),
        name="sums",
    )(*(pltpu.with_memory_space_constraint(x, pltpu.HBM) for x in operands))


def scores_kernel(sample_total, near, far, corner, placed, out_hbm, out, sem):
    tissues, genes, window = out.shape
    blocks = placed.shape[0]
    per_block = genes // blocks
    row, col = iotas(window, window)
    root = 1.0 / (sample_total ** 0.5)

    def piece(b, kind):
        ref, at = (near, 2 * b) if b < blocks else (far, 0)
        return ref[:, at + kind].reshape(window, window)

    def masked(keep, value):
        return jnp.where(keep, value.astype(jnp.float32), 0.0).astype(jnp.bfloat16)

    labelled = [piece(b, 0) for b in range(blocks + 1)]
    banded = [piece(b, 1) for b in range(blocks + 1)]
    diagonal = [masked(col >= row, band) for band in banded]
    beside = [masked(col < row, band) for band in banded[:blocks - 1]] + [corner[...]]
    nothing = jnp.zeros((window, window), jnp.bfloat16)
    pairs, bands = [], []
    for b in range(blocks):
        pairs.append(jnp.concatenate([labelled[b], labelled[b + 1]], axis=0))
        bands.append(jnp.concatenate([
            jnp.concatenate([diagonal[b], beside[b]], axis=1),
            jnp.concatenate([nothing, diagonal[b + 1]], axis=1),
        ], axis=0))

    copies = []
    step = next(n for n in range(min(7, tissues), 0, -1) if tissues % n == 0)
    for t in range(0, tissues, step):
        for b in range(blocks):
            half = placed[b, pl.ds(t * per_block, step * per_block), :]
            top = jnp.dot(half, pairs[b], preferred_element_type=jnp.float32)
            square = jnp.dot(half, bands[b], preferred_element_type=jnp.float32)
            variance = jnp.sum(square * half.astype(jnp.float32), axis=1, keepdims=True)
            scale = lax.rsqrt(jnp.maximum(variance, 0.0) + 1e-06) * root
            out[pl.ds(t, step), pl.ds(b * per_block, per_block), :] = (top * scale).reshape(step, per_block, window)
        part = pl.ds(t, step)
        copies.append(pltpu.make_async_copy(out.at[part], out_hbm.at[part], sem.at[t // step]))
        copies[-1].start()
    for copy in copies:
        copy.wait()


def on_device(genotype, phenotype, residual, sign_flips, weights, member, gene_start, gene_end):
    by_tissue = weights.transpose(1, 0, 2)
    near, far, corner, placed = reduced_sums(
        genotype, phenotype, residual, sign_flips, gene_start, gene_end, member, by_tissue)
    vmem = pl.BlockSpec(memory_space=pltpu.VMEM)
    scores = pl.pallas_call(
        functools.partial(scores_kernel, genotype.shape[0] * lax.axis_size("samp")),
        out_shape=jax.ShapeDtypeStruct(by_tissue.shape, jnp.float32),
        in_specs=[vmem] * 4,
        out_specs=pl.BlockSpec(memory_space=pltpu.HBM),
        scratch_shapes=[
            pltpu.VMEM(by_tissue.shape, jnp.float32),
            pltpu.SemaphoreType.DMA((by_tissue.shape[0],)),
        ],
        compiler_params=pltpu.CompilerParams(vmem_limit_bytes=VMEM_LIMIT),
        name="scores",
    )(near, far, corner, placed)
    return scores.transpose(1, 0, 2)


def solution(mesh):
    return jax.shard_map(
        on_device,
        mesh=mesh,
        in_specs=(
            P("samp", "snp"),
            P("samp"),
            P("samp"),
            P("samp", None),
            P("snp", None, None),
            P("snp", None),
            P("snp"),
            P("snp"),
        ),
        out_specs=P("snp", None, None),
        check_vma=False,
    )
```

time: 21.6 us -> 22.2 us (1.028)
  Pallas kernels: 21.4 us -> 22 us
    pallas_call x1, Pallas kernels: 19.7 us -> 20.3 us  [reduced_sums(): pl.pallas_call(functools.partial(sums_kernel, count, ring, window), out_s...]
where the time goes in v4:
time: 22.2 us; the launch traced here: 22 us
  Pallas kernels  22 us (99%)
    pallas_call x1, Pallas kernels, reduced_sums(): pl.pallas_call(functools.partial(sums_kernel, count, ring, window), out_s...  20.3 us
    pallas_call x1, Pallas kernels, on_device(): pl.pallas_call(functools.partial(scores_kernel, genotype.shape[0] * lax.a...  1.77 us

profile of v4, /device:TPU:1, one launch (start us, length us, event | category | flops | bytes accessed | tf_op | source)
XLA Modules:
  0.0 22.0 jit_solution(14116967117164178598)
XLA Ops:
  0.0 20.3 %sums.1 = (bf16[8,4,16,128]{3,2,1,0:T(8,128)(2,1)S(1)}, bf16[8,2,16,128]{3,2,1,0:T(8,128)(2,1)S(1)}, bf16[128,128]{1,0:T(8,128)(2,1)S(1)}, bf16[2,784,256]{2,1,0:T(8,128)(2,1)S(1)}) custom-call(bf16[2048,256]{1,0:T(8,128)(2,1)} %geno.1, f32[16,128]{1,0:T(8,128)} %bitcast.7, f32[16,128]{1,0:T(8,128)} %bitcast.8, s32[2048,127]{1,0:T(8,128)} %flips.1, ...), custom_call_target="tpu_custom_call" | custom-call | tf_op jit(solution)/shard_map/sums/pallas_call | solution.py:424
  20.3 1.8 %scores.1 = f32[49,32,128]{2,1,0:T(8,128)} custom-call(bf16[8,4,16,128]{3,2,1,0:T(8,128)(2,1)S(1)} %get-tuple-element.9.near, bf16[8,2,16,128]{3,2,1,0:T(8,128)(2,1)S(1)} %get-tuple-element.10.far, bf16[128,128]{1,0:T(8,128)(2,1)S(1)} %get-tuple-element.11.corner, bf16[2,784,256]{2,1,0:T(8,128)(2,1)S(1)} %get-tuple-element.12.placed), custom_call_target="tpu_custom_call" | custom-call | tf_op jit(solution)/shard_map/scores/pallas_call | solution.py:515

commit v5 on v4

--- a/solution.py
+++ b/solution.py
@@ -48,7 +48,7 @@
     sums_s, sums_r, sums_t, cols_v, near_v, next_v,
     load_sem, flip_sem, small_sem, halo_ss, halo_rs,
     ms_ss, ms_rs, mg_ss, mg_rs, lt_ss, lt_rs, bc_ss, bc_rs, td_ss, td_rs,
-    sm_ss, sm_rs, st_ss, st_rs, bk_ss, bk_rs,
+    sm_ss, sm_rs, st_ss, st_rs, bk_ss, bk_rs, fw_ss, fw_rs,
 ):
     me = lax.axis_index("samp")
     mine = lax.axis_index("snp")
@@ -62,8 +62,7 @@
     partner = mine + 1 - 2 * parity
     slot = 1 - parity
     samples = data_v.shape[0]
-    owners, bands, per, _ = main_g.shape
-    blocks = bands // 2
+    blocks, owners, _, per, _ = main_g.shape
     snps = blocks * window
     part = samples // PARTS
     split = samples // HALVES
@@ -162,8 +161,8 @@
         low, mid, high = b * window, (b + 1) * window, (b + 2) * window
         other = products[low:mid, mid:high] if b < blocks - 1 else 0.0
         band = jnp.where(col >= row, products[low:mid, low:mid], other)
-        main_s[:, 2 * b] = products[low:mid, snps:].astype(jnp.bfloat16).reshape(owners, per, window)
-        main_s[:, 2 * b + 1] = band.astype(jnp.bfloat16).reshape(owners, per, window)
+        main_s[b, :, 0] = products[low:mid, snps:].astype(jnp.bfloat16).reshape(owners, per, window)
+        main_s[b, :, 1] = band.astype(jnp.bfloat16).reshape(owners, per, window)
 
     def remote(src, dst, ss, rs, device):
         return pltpu.make_async_remote_copy(
@@ -190,20 +189,22 @@
         return remote(
             sums_s, sums_r.at[slot, dist], sm_ss.at[dist], sm_rs.at[slot, dist], (ahead(dist), keeper))
 
-    def scatter_copy(dist):
+    def scatter_copy(b, dist):
         return remote(
-            main_s.at[ahead(dist)], main_r.at[slot, dist],
-            ms_ss.at[dist], ms_rs.at[slot, dist], (ahead(dist), keeper))
-
-    def gather_copy(s, dist, place):
+            main_s.at[b, ahead(dist)], main_r.at[slot, b, dist],
+            ms_ss.at[b, dist], ms_rs.at[slot, b, dist], (ahead(dist), keeper))
+
+    def gather_copy(s, b, dist, place):
         return remote(
-            main_p.at[s], main_g.at[place], mg_ss.at[s, dist], mg_rs.at[dist],
+            main_p.at[s, b], main_g.at[b, place], mg_ss.at[s, b, dist], mg_rs.at[b, dist],
             (ahead(dist), jnp.maximum(mine - s, 0)))
 
-    def direct_copy(s, dist, place):
+    def direct_copy(dist, place):
         return remote(
-            main_p.at[s, pl.ds(0, 2)], tail_v.at[place], td_ss.at[s, dist], td_rs.at[dist],
-            (ahead(dist), jnp.maximum(mine - 1 - s, 0)))
+            main_p.at[1, 0], tail_v.at[place], td_ss.at[dist], td_rs.at[dist],
+            (ahead(dist), jnp.maximum(mine - 2, 0)))
+
+    forward = remote(main_g.at[0], tail_v, fw_ss.at[0], fw_rs.at[0], (me, before))
 
     def late_copy(dist):
         return remote(late_s, late_r.at[dist], lt_ss.at[dist], lt_rs.at[dist], (ahead(dist), mine))
@@ -231,7 +232,8 @@
 
     pl.when(has_after & odd)(back.start)
     group(lambda dist: sums_copy(dist).start())
-    group(lambda dist: guarded(ahead(dist), lambda: scatter_copy(dist).start()))
+    for b in range(blocks):
+        group(lambda dist: guarded(ahead(dist), lambda: scatter_copy(b, dist).start()))
 
     half = window // 2
     half_row, half_col = iotas(half, window)
@@ -268,33 +270,30 @@
             sums_r.at[s], sums_s[...] if s == 0 else jnp.zeros_like(sums_s), 1 - s)
         cols_v[s] = square_of(sums_t[s]).T
 
-    def own(s):
+    def own(s, b):
         def body():
             total = collect(
                 lambda dist: remote(
-                    main_s.at[0], main_r.at[s, dist], ms_ss.at[dist], ms_rs.at[s, dist],
+                    main_s.at[b, 0], main_r.at[s, b, dist], ms_ss.at[b, dist], ms_rs.at[s, b, dist],
                     (ahead(dist), partner)).wait_recv(),
-                main_r.at[s],
-                main_s[me].astype(jnp.float32) if s == 0 else jnp.zeros(main_p.shape[1:], jnp.float32), 1 - s)
+                main_r.at[s, b],
+                main_s[b, me].astype(jnp.float32) if s == 0 else jnp.zeros(main_p.shape[2:], jnp.float32), 1 - s)
             row_of, col_of = iotas(per, window)
             row_of = row_of + me * per
-            columns = cols_v[s, pl.ds(pl.multiple_of(me * per, per), per), :] * inverse
-            for b in range(blocks):
-                at = columns[:, b:b + 1]
-                scored = total[2 * b] - at * sums_t[s, blocks:blocks + 1, :]
-                main_p[s, 2 * b] = pltpu.roll(scored, 1, 1).astype(main_p.dtype)
-                mean_row = sums_t[s, b:b + 1, :] * inverse
-                if b < blocks - 1:
-                    mean_row = jnp.where(col_of >= row_of, mean_row, sums_t[s, b + 1:b + 2, :] * inverse)
-                value = total[2 * b + 1] * inverse - at * mean_row
-                value = jnp.where(col_of == row_of, value, 2.0 * value)
-                main_p[s, 2 * b + 1] = value.astype(main_p.dtype)
-            peers(lambda dist: gather_copy(s, dist, me).start(), 1 - s)
+            at = cols_v[s, pl.ds(pl.multiple_of(me * per, per), per), :][:, b:b + 1] * inverse
+            scored = total[0] - at * sums_t[s, blocks:blocks + 1, :]
+            main_p[s, b, 0] = pltpu.roll(scored, 1, 1).astype(main_p.dtype)
+            mean_row = sums_t[s, b:b + 1, :] * inverse
+            if b < blocks - 1:
+                mean_row = jnp.where(col_of >= row_of, mean_row, sums_t[s, b + 1:b + 2, :] * inverse)
+            value = total[1] * inverse - at * mean_row
+            value = jnp.where(col_of == row_of, value, 2.0 * value)
+            main_p[s, b, 1] = value.astype(main_p.dtype)
+            if s == 1 and b == 0:
+                pl.when(further)(lambda: peers(lambda dist: direct_copy(dist, me).start(), 0))
+            peers(lambda dist: gather_copy(s, b, dist, me).start(), 1 - s)
             if s == 0:
-                peers(lambda dist: direct_copy(s, dist, me).start(), 0)
-                main_g[me] = main_p[s]
-            else:
-                pl.when(further)(lambda: peers(lambda dist: direct_copy(s, dist, me).start(), 0))
+                main_g[b, me] = main_p[s, b]
         guarded(me, body)
 
     @pl.when(odd)
@@ -304,10 +303,23 @@
         stats[0].start()
         stats[1].start()
         pl.when(further)(stats[2].start)
-        for s in range(2):
-            own(s)
+        for s in (1, 0):
+            own(s, 0)
 
     pl.when(has_after & odd)(lambda: corner(1))
+
+    @pl.when(odd)
+    def _():
+        for b in range(1, blocks):
+            for s in (1, 0):
+                own(s, b)
+
+    def gathered(b):
+        group(lambda dist: guarded(
+            behind(dist), lambda: gather_copy(0, b, dist, behind(dist)).wait_recv()))
+
+    gathered(0)
+    pl.when(odd)(forward.start)
 
     @pl.when(has_after)
     def _():
@@ -336,14 +348,15 @@
         value = product * inverse - mean_col * (next_v[0:1, :] * inverse)
         corner_out[...] = jnp.where(col < row, 2.0 * value, 0.0).astype(corner_out.dtype)
 
-    group(lambda dist: guarded(
-        behind(dist), lambda: gather_copy(0, dist, behind(dist)).wait_recv()))
+    for b in range(1, blocks):
+        gathered(b)
     near_out[...] = main_g[...]
 
     @pl.when(has_after)
     def _():
-        peers(lambda dist: guarded(
-            behind(dist), lambda: direct_copy(0, dist, behind(dist)).wait_recv()), 0)
+        pl.when(even)(forward.wait_recv)
+        pl.when(odd)(lambda: peers(lambda dist: guarded(
+            behind(dist), lambda: direct_copy(dist, behind(dist)).wait_recv()), 0))
         far_out[...] = tail_v[...]
 
     @pl.when(jnp.logical_not(has_after))
@@ -356,7 +369,8 @@
     pl.when(has_after & odd)(back.wait_send)
     pl.when(has_after)(lambda: peers(lambda dist: late_copy(dist).wait_send()))
     group(lambda dist: sums_copy(dist).wait_send())
-    group(lambda dist: guarded(ahead(dist), lambda: scatter_copy(dist).wait_send()))
+    for b in range(blocks):
+        group(lambda dist: guarded(ahead(dist), lambda: scatter_copy(b, dist).wait_send()))
 
     @pl.when(odd)
     def _():
@@ -366,11 +380,13 @@
         stats[1].wait_send()
         pl.when(further)(stats[2].wait_send)
 
+        forward.wait_send()
+
         def sent():
-            for s in range(2):
-                peers(lambda dist: gather_copy(s, dist, me).wait_send(), 1 - s)
-            peers(lambda dist: direct_copy(0, dist, me).wait_send(), 0)
-            pl.when(further)(lambda: peers(lambda dist: direct_copy(1, dist, me).wait_send(), 0))
+            for b in range(blocks):
+                for s in range(2):
+                    peers(lambda dist: gather_copy(s, b, dist, me).wait_send(), 1 - s)
+            pl.when(further)(lambda: peers(lambda dist: direct_copy(dist, me).wait_send(), 0))
         guarded(me, sent)
 
 
@@ -424,7 +440,7 @@
     return pl.pallas_call(
         functools.partial(sums_kernel, count, ring, window),
         out_shape=(
-            jax.ShapeDtypeStruct((owners, 2 * blocks, per, window), half),
+            jax.ShapeDtypeStruct((blocks, owners, 2, per, window), half),
             jax.ShapeDtypeStruct((owners, 2, per, window), half),
             jax.ShapeDtypeStruct((window, window), half),
             jax.ShapeDtypeStruct((blocks, tissues * genes // blocks, 2 * window), half),
@@ -436,10 +452,10 @@
             pltpu.VMEM(sign_flips.shape, jnp.int32),
             pltpu.VMEM((samples, window), half),
             pltpu.VMEM((samples - samples // HALVES, window), half),
-            pltpu.VMEM((owners, 2 * blocks, per, window), half),
-            pltpu.VMEM((2, count, 2 * blocks, per, window), half),
-            pltpu.VMEM((2, 2 * blocks, per, window), half),
-            pltpu.VMEM((owners, 2 * blocks, per, window), half),
+            pltpu.VMEM((blocks, owners, 2, per, window), half),
+            pltpu.VMEM((2, blocks, count, 2, per, window), half),
+            pltpu.VMEM((2, blocks, 2, per, window), half),
+            pltpu.VMEM((blocks, owners, 2, per, window), half),
             pltpu.VMEM((window // 2, window), half),
             pltpu.VMEM((count, window // 2, window), half),
             pltpu.VMEM((window // 2, window), half),
@@ -453,9 +469,9 @@
             pltpu.VMEM((8, window), wide),
             pltpu.VMEM((8, window), wide),
             dma((1,)), dma((PARTS,)), dma((6,)), dma((HALVES,)), dma((HALVES,)),
-            dma((count,)), dma((2, count)), dma((2, count)), dma((count,)),
-            dma((count,)), dma((count,)), dma((count,)), dma((count,)), dma((2, count)), dma((count,)),
-            dma((count,)), dma((2, count)), dma((3,)), dma((3,)), dma((1,)), dma((1,)),
+            dma((blocks, count)), dma((2, blocks, count)), dma((2, blocks, count)), dma((blocks, count)),
+            dma((count,)), dma((count,)), dma((count,)), dma((count,)), dma((count,)), dma((count,)),
+            dma((count,)), dma((2, count)), dma((3,)), dma((3,)), dma((1,)), dma((1,)), dma((1,)), dma((1,)),
         ],
         compiler_params=pltpu.CompilerParams(
             collective_id=0, has_side_effects=True, vmem_limit_bytes=VMEM_LIMIT),
@@ -471,8 +487,8 @@
     root = 1.0 / (sample_total ** 0.5)
 
     def piece(b, kind):
-        ref, at = (near, 2 * b) if b < blocks else (far, 0)
-        return ref[:, at + kind].reshape(window, window)
+        ref = near.at[b] if b < blocks else far
+        return ref[:, kind].reshape(window, window)
 
     def masked(keep, value):
         return jnp.where(keep, value.astype(jnp.float32), 0.0).astype(jnp.bfloat16)

time: 22.2 us -> 20.9 us (0.941)
  the two profiles are of different devices: /device:TPU:1 before, /device:TPU:0 now
where the time goes in v5:
time: 20.9 us; the launch traced here: 20.7 us
  Pallas kernels  20.7 us (99%)
    pallas_call x1, Pallas kernels, reduced_sums(): pl.pallas_call(functools.partial(sums_kernel, count, ring, window), out_s...  18.9 us
    pallas_call x1, Pallas kernels, on_device(): pl.pallas_call(functools.partial(scores_kernel, genotype.shape[0] * lax.a...  1.77 us

profile of v5, /device:TPU:0, one launch (start us, length us, event | category | flops | bytes accessed | tf_op | source)
XLA Modules:
  0.0 20.7 jit_solution(15792516811259028968)
XLA Ops:
  0.0 18.9 %sums.1 = (bf16[2,8,2,16,128]{4,3,2,1,0:T(8,128)(2,1)S(1)}, bf16[8,2,16,128]{3,2,1,0:T(8,128)(2,1)S(1)}, bf16[128,128]{1,0:T(8,128)(2,1)S(1)}, bf16[2,784,256]{2,1,0:T(8,128)(2,1)S(1)}) custom-call(bf16[2048,256]{1,0:T(8,128)(2,1)} %geno.1, f32[16,128]{1,0:T(8,128)} %bitcast.7, f32[16,128]{1,0:T(8,128)} %bitcast.8, s32[2048,127]{1,0:T(8,128)} %flips.1, ...), custom_call_target="tpu_custom_call" | custom-call | tf_op jit(solution)/shard_map/sums/pallas_call | solution.py:440
  19.0 1.8 %scores.1 = f32[49,32,128]{2,1,0:T(8,128)} custom-call(bf16[2,8,2,16,128]{4,3,2,1,0:T(8,128)(2,1)S(1)} %get-tuple-element.9.near, bf16[8,2,16,128]{3,2,1,0:T(8,128)(2,1)S(1)} %get-tuple-element.10.far, bf16[128,128]{1,0:T(8,128)(2,1)S(1)} %get-tuple-element.11.corner, bf16[2,784,256]{2,1,0:T(8,128)(2,1)S(1)} %get-tuple-element.12.placed), custom_call_target="tpu_custom_call" | custom-call | tf_op jit(solution)/shard_map/scores/pallas_call | solution.py:531

commit v6 on v5

--- a/solution.py
+++ b/solution.py
@@ -44,8 +44,8 @@
     phen_v, resid_v, starts_v, ends_v, member_v, weights_v,
     data_v, flips_v, halo_v, back_v,
     main_s, main_r, main_p, main_g,
-    late_s, late_r, back_s, back_r, fold_v, tail_v,
-    sums_s, sums_r, sums_t, cols_v, near_v, next_v,
+    late_s, late_r, back_s, back_r, tail_v,
+    sums_s, sums_r, sums_t, cols_v, next_v,
     load_sem, flip_sem, small_sem, halo_ss, halo_rs,
     ms_ss, ms_rs, mg_ss, mg_rs, lt_ss, lt_rs, bc_ss, bc_rs, td_ss, td_rs,
     sm_ss, sm_rs, st_ss, st_rs, bk_ss, bk_rs, fw_ss, fw_rs,
@@ -151,10 +151,11 @@
     data = data_v[...]
     left = jnp.concatenate([data[:, :snps], jnp.ones((samples, 8), jnp.bfloat16)], axis=1)
     products = across(left, data)
-    row8, _ = iotas(8, window)
-    sums = jnp.zeros((8, window), jnp.float32)
+    kinds = sums_s.shape[0]
+    kind_of, _ = iotas(kinds, window)
+    sums = jnp.zeros((kinds, window), jnp.float32)
     for b in range(blocks + 1):
-        sums = jnp.where(row8 == b, products[snps:, b * window:(b + 1) * window], sums)
+        sums = jnp.where(kind_of == b, products[snps:snps + 1, b * window:(b + 1) * window], sums)
     sums_s[...] = sums
     row, col = iotas(window, window)
     for b in range(blocks):
@@ -212,11 +213,7 @@
     def back_copy(dist):
         return remote(back_s, back_r.at[dist], bc_ss.at[dist], bc_rs.at[dist], (ahead(dist), before))
 
-    stats = [
-        remote(sums_t.at[1], near_v, st_ss.at[0], st_rs.at[0], (me, before)),
-        remote(sums_t.at[0], next_v, st_ss.at[1], st_rs.at[1], (me, before)),
-        remote(sums_t.at[1], next_v, st_ss.at[2], st_rs.at[2], (me, jnp.maximum(mine - 2, 0))),
-    ]
+    stats = remote(sums_t.at[1], next_v, st_ss.at[0], st_rs.at[0], (me, jnp.maximum(mine - 2, 0)))
     further = odd & (mine > 1)
 
     pl.semaphore_wait(
@@ -232,8 +229,18 @@
 
     pl.when(has_after & odd)(back.start)
     group(lambda dist: sums_copy(dist).start())
-    for b in range(blocks):
+    for b in range(blocks - 1):
         group(lambda dist: guarded(ahead(dist), lambda: scatter_copy(b, dist).start()))
+
+    @pl.when(even)
+    def _():
+        for copy in halos:
+            copy.wait_recv()
+        beside = across(data_v[:, pl.ds(snps - window, window)], halo_v[...])
+        band = jnp.where(col >= row, main_s[blocks - 1, :, 1].reshape(window, window).astype(jnp.float32), beside)
+        main_s[blocks - 1, :, 1] = band.astype(jnp.bfloat16).reshape(owners, per, window)
+
+    group(lambda dist: guarded(ahead(dist), lambda: scatter_copy(blocks - 1, dist).start()))
 
     half = window // 2
     half_row, half_col = iotas(half, window)
@@ -243,14 +250,11 @@
         folded = jnp.where(half_col - half > half_row, product.T[half:], turned)
         return jnp.where(half_col < half, product[half:], folded).astype(jnp.bfloat16)
 
-    def corner(arrived):
-        for copy in halos[:arrived]:
-            copy.wait_recv()
-        rows = pl.ds(0, arrived * split)
+    def corner():
+        halos[0].wait_recv()
+        rows = pl.ds(0, split)
         late_s[...] = fold(across(data_v[rows, pl.ds(snps - window, window)], halo_v[rows, :]))
         peers(lambda dist: late_copy(dist).start())
-
-    pl.when(even)(lambda: corner(HALVES))
 
     for copy in small[2:]:
         copy.wait()
@@ -283,9 +287,8 @@
             at = cols_v[s, pl.ds(pl.multiple_of(me * per, per), per), :][:, b:b + 1] * inverse
             scored = total[0] - at * sums_t[s, blocks:blocks + 1, :]
             main_p[s, b, 0] = pltpu.roll(scored, 1, 1).astype(main_p.dtype)
-            mean_row = sums_t[s, b:b + 1, :] * inverse
-            if b < blocks - 1:
-                mean_row = jnp.where(col_of >= row_of, mean_row, sums_t[s, b + 1:b + 2, :] * inverse)
+            other = sums_t[s, b + 1:b + 2, :] if b < blocks - 1 else sums_t[0, 0:1, :]
+            mean_row = jnp.where(col_of >= row_of, sums_t[s, b:b + 1, :], other) * inverse
             value = total[1] * inverse - at * mean_row
             value = jnp.where(col_of == row_of, value, 2.0 * value)
             main_p[s, b, 1] = value.astype(main_p.dtype)
@@ -300,19 +303,13 @@
     def _():
         for s in range(2):
             settle(s)
-        stats[0].start()
-        stats[1].start()
-        pl.when(further)(stats[2].start)
-        for s in (1, 0):
-            own(s, 0)
-
-    pl.when(has_after & odd)(lambda: corner(1))
-
-    @pl.when(odd)
-    def _():
-        for b in range(1, blocks):
-            for s in (1, 0):
-                own(s, b)
+        pl.when(further)(stats.start)
+        for b in range(blocks - 1):
+            own(1, b)
+            own(0, b)
+        own(0, blocks - 1)
+        pl.when(has_after)(corner)
+        own(1, blocks - 1)
 
     def gathered(b):
         group(lambda dist: guarded(
@@ -321,30 +318,16 @@
     gathered(0)
     pl.when(odd)(forward.start)
 
-    @pl.when(has_after)
-    def _():
-        @pl.when(even)
-        def _():
-            stats[0].wait_recv()
-            stats[1].wait_recv()
-
-        @pl.when(odd)
-        def _():
-            near_v[...] = sums_t[0]
-            stats[2].wait_recv()
-
-        fold_v[...] = collect(
+    @pl.when(has_after & odd)
+    def _():
+        stats.wait_recv()
+        folded = collect(
             lambda dist: late_copy(dist).wait_recv(), late_r, late_s[...].astype(jnp.float32))
-
-        @pl.when(odd)
-        def _():
-            fold_v[...] = collect(lambda dist: back_copy(dist).wait_recv(), back_r, fold_v[...], 0)
-
-        folded = fold_v[...]
+        folded = collect(lambda dist: back_copy(dist).wait_recv(), back_r, folded, 0)
         mirrored = jnp.concatenate([folded, folded], axis=0).T
         product = jnp.concatenate([
             pltpu.roll(folded, half, 1), jnp.where(half_col < half, folded, mirrored[half:])], axis=0)
-        mean_col = square_of(near_v[...]).T[:, blocks - 1:blocks] * inverse
+        mean_col = cols_v[0, :, blocks - 1:blocks] * inverse
         value = product * inverse - mean_col * (next_v[0:1, :] * inverse)
         corner_out[...] = jnp.where(col < row, 2.0 * value, 0.0).astype(corner_out.dtype)
 
@@ -354,7 +337,12 @@
 
     @pl.when(has_after)
     def _():
-        pl.when(even)(forward.wait_recv)
+        @pl.when(even)
+        def _():
+            beside = main_g[blocks - 1, :, 1].reshape(window, window).astype(jnp.float32)
+            corner_out[...] = jnp.where(col < row, beside, 0.0).astype(corner_out.dtype)
+            forward.wait_recv()
+
         pl.when(odd)(lambda: peers(lambda dist: guarded(
             behind(dist), lambda: direct_copy(dist, behind(dist)).wait_recv()), 0))
         far_out[...] = tail_v[...]
@@ -367,7 +355,7 @@
     pl.when(has_before)(halos[0].wait_send)
     pl.when(has_before & even)(lambda: peers(lambda dist: back_copy(dist).wait_send(), 0))
     pl.when(has_after & odd)(back.wait_send)
-    pl.when(has_after)(lambda: peers(lambda dist: late_copy(dist).wait_send()))
+    pl.when(has_after & odd)(lambda: peers(lambda dist: late_copy(dist).wait_send()))
     group(lambda dist: sums_copy(dist).wait_send())
     for b in range(blocks):
         group(lambda dist: guarded(ahead(dist), lambda: scatter_copy(b, dist).wait_send()))
@@ -376,9 +364,7 @@
     def _():
         for copy in halos[1:]:
             copy.wait_send()
-        stats[0].wait_send()
-        stats[1].wait_send()
-        pl.when(further)(stats[2].wait_send)
+        pl.when(further)(stats.wait_send)
 
         forward.wait_send()
 
@@ -429,6 +415,7 @@
     blocks = snps // window
     per = share_of(window, count)
     owners = window // per
+    kinds = -(-(blocks + 1) // 4) * 4
     half, wide = jnp.bfloat16, jnp.float32
     dma = pltpu.SemaphoreType.DMA
     vmem = pl.BlockSpec(memory_space=pltpu.VMEM)
@@ -460,18 +447,16 @@
             pltpu.VMEM((count, window // 2, window), half),
             pltpu.VMEM((window // 2, window), half),
             pltpu.VMEM((count, window // 2, window), half),
-            pltpu.VMEM((window // 2, window), wide),
             pltpu.VMEM((owners, 2, per, window), half),
-            pltpu.VMEM((8, window), wide),
-            pltpu.VMEM((2, count, 8, window), wide),
-            pltpu.VMEM((2, 8, window), wide),
+            pltpu.VMEM((kinds, window), wide),
+            pltpu.VMEM((2, count, kinds, window), wide),
+            pltpu.VMEM((2, kinds, window), wide),
             pltpu.VMEM((2, window, window), wide),
-            pltpu.VMEM((8, window), wide),
-            pltpu.VMEM((8, window), wide),
+            pltpu.VMEM((kinds, window), wide),
             dma((1,)), dma((PARTS,)), dma((6,)), dma((HALVES,)), dma((HALVES,)),
             dma((blocks, count)), dma((2, blocks, count)), dma((2, blocks, count)), dma((blocks, count)),
             dma((count,)), dma((count,)), dma((count,)), dma((count,)), dma((count,)), dma((count,)),
-            dma((count,)), dma((2, count)), dma((3,)), dma((3,)), dma((1,)), dma((1,)), dma((1,)), dma((1,)),
+            dma((count,)), dma((2, count)), dma((1,)), dma((1,)), dma((1,)), dma((1,)), dma((1,)), dma((1,)),
         ],
         compiler_params=pltpu.CompilerParams(
             collective_id=0, has_side_effects=True, vmem_limit_bytes=VMEM_LIMIT),

time: 20.9 us -> 20.8 us (level)
  no operation moved by 1% of the time
where the time goes in v6:
time: 20.8 us; the launch traced here: 20.7 us
  Pallas kernels  20.7 us (100%)
    pallas_call x1, Pallas kernels, reduced_sums(): pl.pallas_call(functools.partial(sums_kernel, count, ring, window), out_s...  18.9 us
    pallas_call x1, Pallas kernels, on_device(): pl.pallas_call(functools.partial(scores_kernel, genotype.shape[0] * lax.a...  1.77 us

profile of v6, /device:TPU:0, one launch (start us, length us, event | category | flops | bytes accessed | tf_op | source)
XLA Modules:
  0.0 20.7 jit_solution(2859964005431071731)
XLA Ops:
  0.0 18.9 %sums.1 = (bf16[2,8,2,16,128]{4,3,2,1,0:T(8,128)(2,1)S(1)}, bf16[8,2,16,128]{3,2,1,0:T(8,128)(2,1)S(1)}, bf16[128,128]{1,0:T(8,128)(2,1)S(1)}, bf16[2,784,256]{2,1,0:T(8,128)(2,1)S(1)}) custom-call(bf16[2048,256]{1,0:T(8,128)(2,1)} %geno.1, f32[16,128]{1,0:T(8,128)} %bitcast.7, f32[16,128]{1,0:T(8,128)} %bitcast.8, s32[2048,127]{1,0:T(8,128)} %flips.1, ...), custom_call_target="tpu_custom_call" | custom-call | tf_op jit(solution)/shard_map/sums/pallas_call | solution.py:427
  18.9 1.8 %scores.1 = f32[49,32,128]{2,1,0:T(8,128)} custom-call(bf16[2,8,2,16,128]{4,3,2,1,0:T(8,128)(2,1)S(1)} %get-tuple-element.9.near, bf16[8,2,16,128]{3,2,1,0:T(8,128)(2,1)S(1)} %get-tuple-element.10.far, bf16[128,128]{1,0:T(8,128)(2,1)S(1)} %get-tuple-element.11.corner, bf16[2,784,256]{2,1,0:T(8,128)(2,1)S(1)} %get-tuple-element.12.placed), custom_call_target="tpu_custom_call" | custom-call | tf_op jit(solution)/shard_map/scores/pallas_call | solution.py:516

commit v7 on v6

--- a/solution.py
+++ b/solution.py
@@ -195,10 +195,25 @@
             main_s.at[b, ahead(dist)], main_r.at[slot, b, dist],
             ms_ss.at[b, dist], ms_rs.at[slot, b, dist], (ahead(dist), keeper))
 
-    def gather_copy(s, b, dist, place):
+    def everyone(body, apart):
+        def one(other):
+            if apart is None:
+                body(other)
+            else:
+                pl.when((other != me) | apart)(lambda: body(other))
+        if count <= 16:
+            for other in range(count):
+                one(other)
+        else:
+            def step(other, carry):
+                one(other)
+                return carry
+            lax.fori_loop(0, count, step, 0)
+
+    def gather_copy(s, b, other, place, source):
         return remote(
-            main_p.at[s, b], main_g.at[b, place], mg_ss.at[s, b, dist], mg_rs.at[b, dist],
-            (ahead(dist), jnp.maximum(mine - s, 0)))
+            main_p.at[s, b], main_g.at[b, place], mg_ss.at[s, b, other], mg_rs.at[b, source],
+            (other, jnp.maximum(mine - s, 0)))
 
     def direct_copy(dist, place):
         return remote(
@@ -294,7 +309,7 @@
             main_p[s, b, 1] = value.astype(main_p.dtype)
             if s == 1 and b == 0:
                 pl.when(further)(lambda: peers(lambda dist: direct_copy(dist, me).start(), 0))
-            peers(lambda dist: gather_copy(s, b, dist, me).start(), 1 - s)
+            everyone(lambda other: gather_copy(s, b, other, me, me).start(), None if s else False)
             if s == 0:
                 main_g[b, me] = main_p[s, b]
         guarded(me, body)
@@ -308,12 +323,34 @@
             own(1, b)
             own(0, b)
         own(0, blocks - 1)
+        own(1, blocks - 1)
         pl.when(has_after)(corner)
-        own(1, blocks - 1)
 
     def gathered(b):
-        group(lambda dist: guarded(
-            behind(dist), lambda: gather_copy(0, b, dist, behind(dist)).wait_recv()))
+        everyone(lambda other: guarded(
+            other, lambda: gather_copy(0, b, other, other, other).wait_recv()), even)
+        near_out[b] = main_g[b]
+
+    pl.when(has_before)(halos[0].wait_send)
+    pl.when(has_before & even)(lambda: peers(lambda dist: back_copy(dist).wait_send(), 0))
+    pl.when(has_after & odd)(back.wait_send)
+    pl.when(has_after & odd)(lambda: peers(lambda dist: late_copy(dist).wait_send()))
+    group(lambda dist: sums_copy(dist).wait_send())
+    for b in range(blocks):
+        group(lambda dist: guarded(ahead(dist), lambda: scatter_copy(b, dist).wait_send()))
+
+    @pl.when(odd)
+    def _():
+        for copy in halos[1:]:
+            copy.wait_send()
+        pl.when(further)(stats.wait_send)
+
+        def sent():
+            for b in range(blocks):
+                for s in range(2):
+                    everyone(lambda other: gather_copy(s, b, other, me, me).wait_send(), None if s else False)
+            pl.when(further)(lambda: peers(lambda dist: direct_copy(dist, me).wait_send(), 0))
+        guarded(me, sent)
 
     gathered(0)
     pl.when(odd)(forward.start)
@@ -333,7 +370,6 @@
 
     for b in range(1, blocks):
         gathered(b)
-    near_out[...] = main_g[...]
 
     @pl.when(has_after)
     def _():
@@ -352,28 +388,7 @@
         corner_out[...] = jnp.zeros_like(corner_out)
         far_out[...] = jnp.zeros_like(far_out)
 
-    pl.when(has_before)(halos[0].wait_send)
-    pl.when(has_before & even)(lambda: peers(lambda dist: back_copy(dist).wait_send(), 0))
-    pl.when(has_after & odd)(back.wait_send)
-    pl.when(has_after & odd)(lambda: peers(lambda dist: late_copy(dist).wait_send()))
-    group(lambda dist: sums_copy(dist).wait_send())
-    for b in range(blocks):
-        group(lambda dist: guarded(ahead(dist), lambda: scatter_copy(b, dist).wait_send()))
-
-    @pl.when(odd)
-    def _():
-        for copy in halos[1:]:
-            copy.wait_send()
-        pl.when(further)(stats.wait_send)
-
-        forward.wait_send()
-
-        def sent():
-            for b in range(blocks):
-                for s in range(2):
-                    peers(lambda dist: gather_copy(s, b, dist, me).wait_send(), 1 - s)
-            pl.when(further)(lambda: peers(lambda dist: direct_copy(dist, me).wait_send(), 0))
-        guarded(me, sent)
+    pl.when(odd)(forward.wait_send)
 
 
 def place(offset, starts, ends, member, weights, placed):

time: 20.8 us -> 19.8 us (0.952); the launches traced: 20.7 us -> 19.5 us
  Pallas kernels: 20.7 us -> 19.5 us
    pallas_call x1, Pallas kernels: 18.9 us -> 17.7 us  [reduced_sums(): pl.pallas_call(functools.partial(sums_kernel, count, ring, window), out_s...]
where the time goes in v7:
time: 19.8 us; the launch traced here: 19.5 us
  Pallas kernels  19.5 us (98%)
    pallas_call x1, Pallas kernels, reduced_sums(): pl.pallas_call(functools.partial(sums_kernel, count, ring, window), out_s...  17.7 us
    pallas_call x1, Pallas kernels, on_device(): pl.pallas_call(functools.partial(scores_kernel, genotype.shape[0] * lax.a...  1.77 us

profile of v7, /device:TPU:0, one launch (start us, length us, event | category | flops | bytes accessed | tf_op | source)
XLA Modules:
  0.0 19.5 jit_solution(14908975651352720606)
XLA Ops:
  0.0 17.7 %sums.1 = (bf16[2,8,2,16,128]{4,3,2,1,0:T(8,128)(2,1)S(1)}, bf16[8,2,16,128]{3,2,1,0:T(8,128)(2,1)S(1)}, bf16[128,128]{1,0:T(8,128)(2,1)S(1)}, bf16[2,784,256]{2,1,0:T(8,128)(2,1)S(1)}) custom-call(bf16[2048,256]{1,0:T(8,128)(2,1)} %geno.1, f32[16,128]{1,0:T(8,128)} %bitcast.7, f32[16,128]{1,0:T(8,128)} %bitcast.8, s32[2048,127]{1,0:T(8,128)} %flips.1, ...), custom_call_target="tpu_custom_call" | custom-call | tf_op jit(solution)/shard_map/sums/pallas_call | solution.py:442
  17.7 1.8 %scores.1 = f32[49,32,128]{2,1,0:T(8,128)} custom-call(bf16[2,8,2,16,128]{4,3,2,1,0:T(8,128)(2,1)S(1)} %get-tuple-element.9.near, bf16[8,2,16,128]{3,2,1,0:T(8,128)(2,1)S(1)} %get-tuple-element.10.far, bf16[128,128]{1,0:T(8,128)(2,1)S(1)} %get-tuple-element.11.corner, bf16[2,784,256]{2,1,0:T(8,128)(2,1)S(1)} %get-tuple-element.12.placed), custom_call_target="tpu_custom_call" | custom-call | tf_op jit(solution)/shard_map/scores/pallas_call | solution.py:531

commit v8 on v7

--- a/solution.py
+++ b/solution.py
@@ -9,7 +9,7 @@
 
 MESH = pl.DeviceIdType.MESH
 TILE = 16
-PARTS = 4
+PARTS = 2
 HALVES = 2
 VMEM_LIMIT = 24 * 1024 * 1024
 
@@ -108,14 +108,20 @@
         ))
     ]
     flip_loads = []
-    for copy in small[:2]:
-        copy.start()
     for i in range(PARTS):
         rows = pl.ds(i * part, part)
         flip_loads.append(pltpu.make_async_copy(flips.at[rows], flips_v.at[rows], flip_sem.at[i]))
-        flip_loads[i].start()
+    for copy in small[:2] + flip_loads:
+        copy.start()
     load = pltpu.make_async_copy(geno, data_v.at[:, pl.ds(0, snps)], load_sem.at[0])
     load.start()
+
+    class Behind:
+        def __init__(self, ref):
+            self.ref = ref
+
+        def __getitem__(self, dist):
+            return self.ref[behind(dist)]
 
     barrier = pltpu.get_barrier_semaphore()
 
@@ -148,22 +154,28 @@
             data_v[rows, pl.ds(snps, window)] = labels.astype(jnp.bfloat16)
 
     load.wait()
-    data = data_v[...]
-    left = jnp.concatenate([data[:, :snps], jnp.ones((samples, 8), jnp.bfloat16)], axis=1)
-    products = across(left, data)
-    kinds = sums_s.shape[0]
-    kind_of, _ = iotas(kinds, window)
-    sums = jnp.zeros((kinds, window), jnp.float32)
-    for b in range(blocks + 1):
-        sums = jnp.where(kind_of == b, products[snps:snps + 1, b * window:(b + 1) * window], sums)
-    sums_s[...] = sums
     row, col = iotas(window, window)
-    for b in range(blocks):
-        low, mid, high = b * window, (b + 1) * window, (b + 2) * window
-        other = products[low:mid, mid:high] if b < blocks - 1 else 0.0
-        band = jnp.where(col >= row, products[low:mid, low:mid], other)
-        main_s[b, :, 0] = products[low:mid, snps:].astype(jnp.bfloat16).reshape(owners, per, window)
+
+    def packed(b):
+        left = data_v[:, pl.ds(b * window, window)]
+        if b == 0:
+            left = jnp.concatenate([left, jnp.ones((samples, 8), jnp.bfloat16)], axis=1)
+        products = across(left, data_v[:, pl.ds(b * window, snps + window - b * window)])
+        other = products[:window, window:2 * window] if b < blocks - 1 else 0.0
+        band = jnp.where(col >= row, products[:window, :window], other)
+        scored = products[:window, snps - b * window:]
+        main_s[b, :, 0] = scored.astype(jnp.bfloat16).reshape(owners, per, window)
         main_s[b, :, 1] = band.astype(jnp.bfloat16).reshape(owners, per, window)
+        if b == 0:
+            kinds = sums_s.shape[0]
+            kind_of, _ = iotas(kinds, window)
+            sums = jnp.zeros((kinds, window), jnp.float32)
+            for at in range(blocks + 1):
+                total = products[window:window + 1, at * window:(at + 1) * window]
+                sums = jnp.where(kind_of == at, total, sums)
+            sums_s[...] = sums
+
+    packed(0)
 
     def remote(src, dst, ss, rs, device):
         return pltpu.make_async_remote_copy(
@@ -222,11 +234,11 @@
 
     forward = remote(main_g.at[0], tail_v, fw_ss.at[0], fw_rs.at[0], (me, before))
 
-    def late_copy(dist):
-        return remote(late_s, late_r.at[dist], lt_ss.at[dist], lt_rs.at[dist], (ahead(dist), mine))
-
-    def back_copy(dist):
-        return remote(back_s, back_r.at[dist], bc_ss.at[dist], bc_rs.at[dist], (ahead(dist), before))
+    def late_copy(other, source):
+        return remote(late_s, late_r.at[source], lt_ss.at[other], lt_rs.at[source], (other, mine))
+
+    def back_copy(other, source):
+        return remote(back_s, back_r.at[source], bc_ss.at[other], bc_rs.at[source], (other, before))
 
     stats = remote(sums_t.at[1], next_v, st_ss.at[0], st_rs.at[0], (me, jnp.maximum(mine - 2, 0)))
     further = odd & (mine > 1)
@@ -246,6 +258,7 @@
     group(lambda dist: sums_copy(dist).start())
     for b in range(blocks - 1):
         group(lambda dist: guarded(ahead(dist), lambda: scatter_copy(b, dist).start()))
+        packed(b + 1)
 
     @pl.when(even)
     def _():
@@ -269,7 +282,7 @@
         halos[0].wait_recv()
         rows = pl.ds(0, split)
         late_s[...] = fold(across(data_v[rows, pl.ds(snps - window, window)], halo_v[rows, :]))
-        peers(lambda dist: late_copy(dist).start())
+        everyone(lambda other: late_copy(other, me).start(), False)
 
     for copy in small[2:]:
         copy.wait()
@@ -279,7 +292,7 @@
     def _():
         back.wait_recv()
         back_s[...] = fold(across(back_v[...], data_v[pl.ds(split, samples - split), pl.ds(0, window)]))
-        peers(lambda dist: back_copy(dist).start(), 0)
+        everyone(lambda other: back_copy(other, me).start(), None)
 
     def settle(s):
         sums_t[s] = collect(
@@ -332,9 +345,9 @@
         near_out[b] = main_g[b]
 
     pl.when(has_before)(halos[0].wait_send)
-    pl.when(has_before & even)(lambda: peers(lambda dist: back_copy(dist).wait_send(), 0))
+    pl.when(has_before & even)(lambda: everyone(lambda other: back_copy(other, me).wait_send(), None))
     pl.when(has_after & odd)(back.wait_send)
-    pl.when(has_after & odd)(lambda: peers(lambda dist: late_copy(dist).wait_send()))
+    pl.when(has_after & odd)(lambda: everyone(lambda other: late_copy(other, me).wait_send(), False))
     group(lambda dist: sums_copy(dist).wait_send())
     for b in range(blocks):
         group(lambda dist: guarded(ahead(dist), lambda: scatter_copy(b, dist).wait_send()))
@@ -359,8 +372,9 @@
     def _():
         stats.wait_recv()
         folded = collect(
-            lambda dist: late_copy(dist).wait_recv(), late_r, late_s[...].astype(jnp.float32))
-        folded = collect(lambda dist: back_copy(dist).wait_recv(), back_r, folded, 0)
+            lambda dist: late_copy(behind(dist), behind(dist)).wait_recv(), Behind(late_r),
+            late_s[...].astype(jnp.float32))
+        folded = collect(lambda other: back_copy(other, other).wait_recv(), back_r, folded, 0)
         mirrored = jnp.concatenate([folded, folded], axis=0).T
         product = jnp.concatenate([
             pltpu.roll(folded, half, 1), jnp.where(half_col < half, folded, mirrored[half:])], axis=0)

time: 19.8 us -> 19.8 us (level)
  no operation moved by 1% of the time
where the time goes in v8:
time: 19.8 us; the launch traced here: 19.5 us
  Pallas kernels  19.5 us (98%)
    pallas_call x1, Pallas kernels, reduced_sums(): pl.pallas_call(functools.partial(sums_kernel, count, ring, window), out_s...  17.7 us
    pallas_call x1, Pallas kernels, on_device(): pl.pallas_call(functools.partial(scores_kernel, genotype.shape[0] * lax.a...  1.77 us

profile of v8, /device:TPU:0, one launch (start us, length us, event | category | flops | bytes accessed | tf_op | source)
XLA Modules:
  0.0 19.5 jit_solution(1641151827916860677)
XLA Ops:
  0.0 17.7 %sums.1 = (bf16[2,8,2,16,128]{4,3,2,1,0:T(8,128)(2,1)S(1)}, bf16[8,2,16,128]{3,2,1,0:T(8,128)(2,1)S(1)}, bf16[128,128]{1,0:T(8,128)(2,1)S(1)}, bf16[2,784,256]{2,1,0:T(8,128)(2,1)S(1)}) custom-call(bf16[2048,256]{1,0:T(8,128)(2,1)} %geno.1, f32[16,128]{1,0:T(8,128)} %bitcast.7, f32[16,128]{1,0:T(8,128)} %bitcast.8, s32[2048,127]{1,0:T(8,128)} %flips.1, ...), custom_call_target="tpu_custom_call" | custom-call | tf_op jit(solution)/shard_map/sums/pallas_call | solution.py:456
  17.7 1.8 %scores.1 = f32[49,32,128]{2,1,0:T(8,128)} custom-call(bf16[2,8,2,16,128]{4,3,2,1,0:T(8,128)(2,1)S(1)} %get-tuple-element.9.near, bf16[8,2,16,128]{3,2,1,0:T(8,128)(2,1)S(1)} %get-tuple-element.10.far, bf16[128,128]{1,0:T(8,128)(2,1)S(1)} %get-tuple-element.11.corner, bf16[2,784,256]{2,1,0:T(8,128)(2,1)S(1)} %get-tuple-element.12.placed), custom_call_target="tpu_custom_call" | custom-call | tf_op jit(solution)/shard_map/scores/pallas_call | solution.py:545

commit v9 on v8

--- a/solution.py
+++ b/solution.py
@@ -45,10 +45,10 @@
     data_v, flips_v, halo_v, back_v,
     main_s, main_r, main_p, main_g,
     late_s, late_r, back_s, back_r, tail_v,
-    sums_s, sums_r, sums_t, cols_v, next_v,
+    sums_s, sums_r, sums_t, cols_v, near_v, next_v,
     load_sem, flip_sem, small_sem, halo_ss, halo_rs,
     ms_ss, ms_rs, mg_ss, mg_rs, lt_ss, lt_rs, bc_ss, bc_rs, td_ss, td_rs,
-    sm_ss, sm_rs, st_ss, st_rs, bk_ss, bk_rs, fw_ss, fw_rs,
+    sm_ss, sm_rs, st_ss, st_rs, nr_ss, nr_rs, bk_ss, bk_rs, fw_ss, fw_rs,
 ):
     me = lax.axis_index("samp")
     mine = lax.axis_index("snp")
@@ -58,9 +58,7 @@
     before = jnp.maximum(mine - 1, 0)
     after = jnp.minimum(mine + 1, ring - 1)
     beyond = jnp.minimum(mine + 2, ring - 1)
-    keeper = mine + 1 - parity
     partner = mine + 1 - 2 * parity
-    slot = 1 - parity
     samples = data_v.shape[0]
     blocks, owners, _, per, _ = main_g.shape
     snps = blocks * window
@@ -77,10 +75,6 @@
                 body(dist)
                 return carry
             lax.fori_loop(first, count, step, 0)
-
-    def group(body):
-        pl.when(even)(lambda: body(0))
-        peers(body)
 
     def collect(wait, got, total, first=1):
         if count <= 16:
@@ -128,12 +122,12 @@
     def greet(dist, other):
         pl.semaphore_signal(barrier, inc=1, device_id=(ahead(dist), other), device_id_type=MESH)
 
-    peers(lambda dist: greet(dist, mine))
     peers(lambda dist: greet(dist, partner), 0)
     pl.when(has_before & even)(lambda: greet(0, before))
 
     @pl.when(has_after & odd)
     def _():
+        peers(lambda dist: greet(dist, mine))
         peers(lambda dist: greet(dist, after), 0)
         peers(lambda dist: greet(dist, beyond), 0)
 
@@ -199,13 +193,12 @@
             pl.when(index < owners)(body)
 
     def sums_copy(dist):
-        return remote(
-            sums_s, sums_r.at[slot, dist], sm_ss.at[dist], sm_rs.at[slot, dist], (ahead(dist), keeper))
+        return remote(sums_s, sums_r.at[dist], sm_ss.at[dist], sm_rs.at[dist], (ahead(dist), partner))
 
     def scatter_copy(b, dist):
         return remote(
-            main_s.at[b, ahead(dist)], main_r.at[slot, b, dist],
-            ms_ss.at[b, dist], ms_rs.at[slot, b, dist], (ahead(dist), keeper))
+            main_s.at[b, ahead(dist)], main_r.at[b, dist],
+            ms_ss.at[b, dist], ms_rs.at[b, dist], (ahead(dist), partner))
 
     def everyone(body, apart):
         def one(other):
@@ -222,14 +215,13 @@
                 return carry
             lax.fori_loop(0, count, step, 0)
 
-    def gather_copy(s, b, other, place, source):
+    def gather_copy(b, other, place, source):
         return remote(
-            main_p.at[s, b], main_g.at[b, place], mg_ss.at[s, b, other], mg_rs.at[b, source],
-            (other, jnp.maximum(mine - s, 0)))
+            main_p.at[b], main_g.at[b, place], mg_ss.at[b, other], mg_rs.at[b, source], (other, partner))
 
     def direct_copy(dist, place):
         return remote(
-            main_p.at[1, 0], tail_v.at[place], td_ss.at[dist], td_rs.at[dist],
+            main_p.at[0], tail_v.at[place], td_ss.at[dist], td_rs.at[dist],
             (ahead(dist), jnp.maximum(mine - 2, 0)))
 
     forward = remote(main_g.at[0], tail_v, fw_ss.at[0], fw_rs.at[0], (me, before))
@@ -240,13 +232,14 @@
     def back_copy(other, source):
         return remote(back_s, back_r.at[source], bc_ss.at[other], bc_rs.at[source], (other, before))
 
-    stats = remote(sums_t.at[1], next_v, st_ss.at[0], st_rs.at[0], (me, jnp.maximum(mine - 2, 0)))
+    stats = remote(sums_t, next_v, st_ss.at[0], st_rs.at[0], (me, jnp.maximum(mine - 2, 0)))
+    near = remote(sums_t, near_v, nr_ss.at[0], nr_rs.at[0], (me, partner))
     further = odd & (mine > 1)
 
     pl.semaphore_wait(
         barrier,
-        2 * count - 1 + jnp.where(has_before & even, count, 0)
-        + jnp.where(has_after & odd, 1, 0) + jnp.where(further, count, 0))
+        count + jnp.where(has_before & even, count, 0)
+        + jnp.where(has_after & odd, count, 0) + jnp.where(further, count, 0))
     pl.when(has_before)(halos[0].start)
 
     @pl.when(has_before & odd)
@@ -255,9 +248,9 @@
             copy.start()
 
     pl.when(has_after & odd)(back.start)
-    group(lambda dist: sums_copy(dist).start())
+    peers(lambda dist: sums_copy(dist).start(), 0)
     for b in range(blocks - 1):
-        group(lambda dist: guarded(ahead(dist), lambda: scatter_copy(b, dist).start()))
+        peers(lambda dist: guarded(ahead(dist), lambda: scatter_copy(b, dist).start()), 0)
         packed(b + 1)
 
     @pl.when(even)
@@ -268,7 +261,7 @@
         band = jnp.where(col >= row, main_s[blocks - 1, :, 1].reshape(window, window).astype(jnp.float32), beside)
         main_s[blocks - 1, :, 1] = band.astype(jnp.bfloat16).reshape(owners, per, window)
 
-    group(lambda dist: guarded(ahead(dist), lambda: scatter_copy(blocks - 1, dist).start()))
+    peers(lambda dist: guarded(ahead(dist), lambda: scatter_copy(blocks - 1, dist).start()), 0)
 
     half = window // 2
     half_row, half_col = iotas(half, window)
@@ -294,63 +287,58 @@
         back_s[...] = fold(across(back_v[...], data_v[pl.ds(split, samples - split), pl.ds(0, window)]))
         everyone(lambda other: back_copy(other, me).start(), None)
 
-    def settle(s):
-        sums_t[s] = collect(
-            lambda dist: remote(
-                sums_s, sums_r.at[s, dist], sm_ss.at[dist], sm_rs.at[s, dist],
-                (ahead(dist), partner)).wait_recv(),
-            sums_r.at[s], sums_s[...] if s == 0 else jnp.zeros_like(sums_s), 1 - s)
-        cols_v[s] = square_of(sums_t[s]).T
-
-    def own(s, b):
+    sums_t[...] = collect(
+        lambda dist: sums_copy(dist).wait_recv(), sums_r, jnp.zeros(sums_t.shape, jnp.float32), 0)
+    cols_v[...] = square_of(sums_t[...]).T
+    pl.when(even)(near.start)
+    pl.when(further)(stats.start)
+
+    def own(b):
         def body():
             total = collect(
-                lambda dist: remote(
-                    main_s.at[b, 0], main_r.at[s, b, dist], ms_ss.at[b, dist], ms_rs.at[s, b, dist],
-                    (ahead(dist), partner)).wait_recv(),
-                main_r.at[s, b],
-                main_s[b, me].astype(jnp.float32) if s == 0 else jnp.zeros(main_p.shape[2:], jnp.float32), 1 - s)
+                lambda dist: scatter_copy(b, dist).wait_recv(), main_r.at[b],
+                jnp.zeros(main_p.shape[1:], jnp.float32), 0)
             row_of, col_of = iotas(per, window)
             row_of = row_of + me * per
-            at = cols_v[s, pl.ds(pl.multiple_of(me * per, per), per), :][:, b:b + 1] * inverse
-            scored = total[0] - at * sums_t[s, blocks:blocks + 1, :]
-            main_p[s, b, 0] = pltpu.roll(scored, 1, 1).astype(main_p.dtype)
-            other = sums_t[s, b + 1:b + 2, :] if b < blocks - 1 else sums_t[0, 0:1, :]
-            mean_row = jnp.where(col_of >= row_of, sums_t[s, b:b + 1, :], other) * inverse
+            at = cols_v[pl.ds(pl.multiple_of(me * per, per), per), :][:, b:b + 1] * inverse
+            scored = total[0] - at * sums_t[blocks:blocks + 1, :]
+            main_p[b, 0] = pltpu.roll(scored, 1, 1).astype(main_p.dtype)
+            other = sums_t[b + 1:b + 2, :] if b < blocks - 1 else near_v[0:1, :]
+            mean_row = jnp.where(col_of >= row_of, sums_t[b:b + 1, :], other) * inverse
             value = total[1] * inverse - at * mean_row
             value = jnp.where(col_of == row_of, value, 2.0 * value)
-            main_p[s, b, 1] = value.astype(main_p.dtype)
-            if s == 1 and b == 0:
+            main_p[b, 1] = value.astype(main_p.dtype)
+            if b == 0:
                 pl.when(further)(lambda: peers(lambda dist: direct_copy(dist, me).start(), 0))
-            everyone(lambda other: gather_copy(s, b, other, me, me).start(), None if s else False)
-            if s == 0:
-                main_g[b, me] = main_p[s, b]
+            everyone(lambda other: gather_copy(b, other, me, me).start(), None)
         guarded(me, body)
 
+    for b in range(blocks - 1):
+        own(b)
+    pl.when(has_after & odd)(corner)
+
     @pl.when(odd)
     def _():
-        for s in range(2):
-            settle(s)
-        pl.when(further)(stats.start)
-        for b in range(blocks - 1):
-            own(1, b)
-            own(0, b)
-        own(0, blocks - 1)
-        own(1, blocks - 1)
-        pl.when(has_after)(corner)
+        near.wait_recv()
+
+    @pl.when(even)
+    def _():
+        near_v[...] = jnp.zeros_like(near_v)
+
+    own(blocks - 1)
 
     def gathered(b):
         everyone(lambda other: guarded(
-            other, lambda: gather_copy(0, b, other, other, other).wait_recv()), even)
+            other, lambda: gather_copy(b, other, other, other).wait_recv()), None)
         near_out[b] = main_g[b]
 
     pl.when(has_before)(halos[0].wait_send)
     pl.when(has_before & even)(lambda: everyone(lambda other: back_copy(other, me).wait_send(), None))
     pl.when(has_after & odd)(back.wait_send)
     pl.when(has_after & odd)(lambda: everyone(lambda other: late_copy(other, me).wait_send(), False))
-    group(lambda dist: sums_copy(dist).wait_send())
+    peers(lambda dist: sums_copy(dist).wait_send(), 0)
     for b in range(blocks):
-        group(lambda dist: guarded(ahead(dist), lambda: scatter_copy(b, dist).wait_send()))
+        peers(lambda dist: guarded(ahead(dist), lambda: scatter_copy(b, dist).wait_send()), 0)
 
     @pl.when(odd)
     def _():
@@ -358,12 +346,13 @@
             copy.wait_send()
         pl.when(further)(stats.wait_send)
 
-        def sent():
-            for b in range(blocks):
-                for s in range(2):
-                    everyone(lambda other: gather_copy(s, b, other, me, me).wait_send(), None if s else False)
-            pl.when(further)(lambda: peers(lambda dist: direct_copy(dist, me).wait_send(), 0))
-        guarded(me, sent)
+    pl.when(even)(near.wait_send)
+
+    def sent():
+        for b in range(blocks):
+            everyone(lambda other: gather_copy(b, other, me, me).wait_send(), None)
+        pl.when(further)(lambda: peers(lambda dist: direct_copy(dist, me).wait_send(), 0))
+    guarded(me, sent)
 
     gathered(0)
     pl.when(odd)(forward.start)
@@ -378,7 +367,7 @@
         mirrored = jnp.concatenate([folded, folded], axis=0).T
         product = jnp.concatenate([
             pltpu.roll(folded, half, 1), jnp.where(half_col < half, folded, mirrored[half:])], axis=0)
-        mean_col = cols_v[0, :, blocks - 1:blocks] * inverse
+        mean_col = square_of(near_v[...]).T[:, blocks - 1:blocks] * inverse
         value = product * inverse - mean_col * (next_v[0:1, :] * inverse)
         corner_out[...] = jnp.where(col < row, 2.0 * value, 0.0).astype(corner_out.dtype)
 
@@ -469,8 +458,8 @@
             pltpu.VMEM((samples, window), half),
             pltpu.VMEM((samples - samples // HALVES, window), half),
             pltpu.VMEM((blocks, owners, 2, per, window), half),
-            pltpu.VMEM((2, blocks, count, 2, per, window), half),
-            pltpu.VMEM((2, blocks, 2, per, window), half),
+            pltpu.VMEM((blocks, count, 2, per, window), half),
+            pltpu.VMEM((blocks, 2, per, window), half),
             pltpu.VMEM((blocks, owners, 2, per, window), half),
             pltpu.VMEM((window // 2, window), half),
             pltpu.VMEM((count, window // 2, window), half),
@@ -478,14 +467,16 @@
             pltpu.VMEM((count, window // 2, window), half),
             pltpu.VMEM((owners, 2, per, window), half),
             pltpu.VMEM((kinds, window), wide),
-            pltpu.VMEM((2, count, kinds, window), wide),
-            pltpu.VMEM((2, kinds, window), wide),
-            pltpu.VMEM((2, window, window), wide),
+            pltpu.VMEM((count, kinds, window), wide),
+            pltpu.VMEM((kinds, window), wide),
+            pltpu.VMEM((window, window), wide),
+            pltpu.VMEM((kinds, window), wide),
             pltpu.VMEM((kinds, window), wide),
             dma((1,)), dma((PARTS,)), dma((6,)), dma((HALVES,)), dma((HALVES,)),
-            dma((blocks, count)), dma((2, blocks, count)), dma((2, blocks, count)), dma((blocks, count)),
+            dma((blocks, count)), dma((blocks, count)), dma((blocks, count)), dma((blocks, count)),
             dma((count,)), dma((count,)), dma((count,)), dma((count,)), dma((count,)), dma((count,)),
-            dma((count,)), dma((2, count)), dma((1,)), dma((1,)), dma((1,)), dma((1,)), dma((1,)), dma((1,)),
+            dma((count,)), dma((count,)), dma((1,)), dma((1,)), dma((1,)), dma((1,)),
+            dma((1,)), dma((1,)), dma((1,)), dma((1,)),
         ],
         compiler_params=pltpu.CompilerParams(
             collective_id=0, has_side_effects=True, vmem_limit_bytes=VMEM_LIMIT),

time: 19.8 us -> 20.7 us (1.045)
  Pallas kernels: 19.5 us -> 20.5 us
    pallas_call x1, Pallas kernels: 17.7 us -> 18.7 us  [reduced_sums(): pl.pallas_call(functools.partial(sums_kernel, count, ring, window), out_s...]
where the time goes in v9:
time: 20.7 us; the launch traced here: 20.5 us
  Pallas kernels  20.5 us (99%)
    pallas_call x1, Pallas kernels, reduced_sums(): pl.pallas_call(functools.partial(sums_kernel, count, ring, window), out_s...  18.7 us
    pallas_call x1, Pallas kernels, on_device(): pl.pallas_call(functools.partial(scores_kernel, genotype.shape[0] * lax.a...  1.77 us

profile of v9, /device:TPU:0, one launch (start us, length us, event | category | flops | bytes accessed | tf_op | source)
XLA Modules:
  0.0 20.5 jit_solution(18222467876182810906)
XLA Ops:
  0.0 18.7 %sums.1 = (bf16[2,8,2,16,128]{4,3,2,1,0:T(8,128)(2,1)S(1)}, bf16[8,2,16,128]{3,2,1,0:T(8,128)(2,1)S(1)}, bf16[128,128]{1,0:T(8,128)(2,1)S(1)}, bf16[2,784,256]{2,1,0:T(8,128)(2,1)S(1)}) custom-call(bf16[2048,256]{1,0:T(8,128)(2,1)} %geno.1, f32[16,128]{1,0:T(8,128)} %bitcast.7, f32[16,128]{1,0:T(8,128)} %bitcast.8, s32[2048,127]{1,0:T(8,128)} %flips.1, ...), custom_call_target="tpu_custom_call" | custom-call | tf_op jit(solution)/shard_map/sums/pallas_call | solution.py:445
  18.7 1.8 %scores.1 = f32[49,32,128]{2,1,0:T(8,128)} custom-call(bf16[2,8,2,16,128]{4,3,2,1,0:T(8,128)(2,1)S(1)} %get-tuple-element.9.near, bf16[8,2,16,128]{3,2,1,0:T(8,128)(2,1)S(1)} %get-tuple-element.10.far, bf16[128,128]{1,0:T(8,128)(2,1)S(1)} %get-tuple-element.11.corner, bf16[2,784,256]{2,1,0:T(8,128)(2,1)S(1)} %get-tuple-element.12.placed), custom_call_target="tpu_custom_call" | custom-call | tf_op jit(solution)/shard_map/scores/pallas_call | solution.py:536

commit v10 on v9

--- a/solution.py
+++ b/solution.py
@@ -200,20 +200,20 @@
             main_s.at[b, ahead(dist)], main_r.at[b, dist],
             ms_ss.at[b, dist], ms_rs.at[b, dist], (ahead(dist), partner))
 
-    def everyone(body, apart):
+    def everyone(body, apart, low=0, high=count):
         def one(other):
             if apart is None:
                 body(other)
             else:
                 pl.when((other != me) | apart)(lambda: body(other))
         if count <= 16:
-            for other in range(count):
+            for other in range(low, high):
                 one(other)
         else:
             def step(other, carry):
                 one(other)
                 return carry
-            lax.fori_loop(0, count, step, 0)
+            lax.fori_loop(low, high, step, 0)
 
     def gather_copy(b, other, place, source):
         return remote(
@@ -263,6 +263,7 @@
 
     peers(lambda dist: guarded(ahead(dist), lambda: scatter_copy(blocks - 1, dist).start()), 0)
 
+    soon = max(1, count // 8)
     half = window // 2
     half_row, half_col = iotas(half, window)
 
@@ -275,7 +276,7 @@
         halos[0].wait_recv()
         rows = pl.ds(0, split)
         late_s[...] = fold(across(data_v[rows, pl.ds(snps - window, window)], halo_v[rows, :]))
-        everyone(lambda other: late_copy(other, me).start(), False)
+        everyone(lambda other: late_copy(other, me).start(), False, 0, soon)
 
     for copy in small[2:]:
         copy.wait()
@@ -326,6 +327,7 @@
         near_v[...] = jnp.zeros_like(near_v)
 
     own(blocks - 1)
+    pl.when(has_after & odd)(lambda: everyone(lambda other: late_copy(other, me).start(), False, soon))
 
     def gathered(b):
         everyone(lambda other: guarded(

time: 20.7 us -> 19.5 us (0.942)
  Pallas kernels: 20.5 us -> 19.1 us
    pallas_call x1, Pallas kernels: 18.7 us -> 17.4 us  [reduced_sums(): pl.pallas_call(functools.partial(sums_kernel, count, ring, window), out_s...]
where the time goes in v10:
time: 19.5 us; the launch traced here: 19.2 us
  Pallas kernels  19.1 us (98%)
    pallas_call x1, Pallas kernels, reduced_sums(): pl.pallas_call(functools.partial(sums_kernel, count, ring, window), out_s...  17.4 us
    pallas_call x1, Pallas kernels, on_device(): pl.pallas_call(functools.partial(scores_kernel, genotype.shape[0] * lax.a...  1.77 us

profile of v10, /device:TPU:0, one launch (start us, length us, event | category | flops | bytes accessed | tf_op | source)
XLA Modules:
  0.0 19.2 jit_solution(17415114846086220131)
XLA Ops:
  0.0 17.4 %sums.1 = (bf16[2,8,2,16,128]{4,3,2,1,0:T(8,128)(2,1)S(1)}, bf16[8,2,16,128]{3,2,1,0:T(8,128)(2,1)S(1)}, bf16[128,128]{1,0:T(8,128)(2,1)S(1)}, bf16[2,784,256]{2,1,0:T(8,128)(2,1)S(1)}) custom-call(bf16[2048,256]{1,0:T(8,128)(2,1)} %geno.1, f32[16,128]{1,0:T(8,128)} %bitcast.7, f32[16,128]{1,0:T(8,128)} %bitcast.8, s32[2048,127]{1,0:T(8,128)} %flips.1, ...), custom_call_target="tpu_custom_call" | custom-call | tf_op jit(solution)/shard_map/sums/pallas_call | solution.py:447
  17.4 1.8 %scores.1 = f32[49,32,128]{2,1,0:T(8,128)} custom-call(bf16[2,8,2,16,128]{4,3,2,1,0:T(8,128)(2,1)S(1)} %get-tuple-element.9.near, bf16[8,2,16,128]{3,2,1,0:T(8,128)(2,1)S(1)} %get-tuple-element.10.far, bf16[128,128]{1,0:T(8,128)(2,1)S(1)} %get-tuple-element.11.corner, bf16[2,784,256]{2,1,0:T(8,128)(2,1)S(1)} %get-tuple-element.12.placed), custom_call_target="tpu_custom_call" | custom-call | tf_op jit(solution)/shard_map/scores/pallas_call | solution.py:538

commit v11 on v10

--- a/solution.py
+++ b/solution.py
@@ -219,10 +219,10 @@
         return remote(
             main_p.at[b], main_g.at[b, place], mg_ss.at[b, other], mg_rs.at[b, source], (other, partner))
 
-    def direct_copy(dist, place):
+    def direct_copy(other, place, source):
         return remote(
-            main_p.at[0], tail_v.at[place], td_ss.at[dist], td_rs.at[dist],
-            (ahead(dist), jnp.maximum(mine - 2, 0)))
+            main_p.at[0], tail_v.at[place], td_ss.at[other], td_rs.at[source],
+            (other, jnp.maximum(mine - 2, 0)))
 
     forward = remote(main_g.at[0], tail_v, fw_ss.at[0], fw_rs.at[0], (me, before))
 
@@ -282,17 +282,14 @@
         copy.wait()
     place(mine * snps, starts_v, ends_v, member_v, weights_v, placed_out)
 
-    @pl.when(has_before & even)
-    def _():
-        back.wait_recv()
-        back_s[...] = fold(across(back_v[...], data_v[pl.ds(split, samples - split), pl.ds(0, window)]))
-        everyone(lambda other: back_copy(other, me).start(), None)
-
     sums_t[...] = collect(
         lambda dist: sums_copy(dist).wait_recv(), sums_r, jnp.zeros(sums_t.shape, jnp.float32), 0)
     cols_v[...] = square_of(sums_t[...]).T
     pl.when(even)(near.start)
     pl.when(further)(stats.start)
+
+    def direct(low, high):
+        everyone(lambda other: direct_copy(other, me, me).start(), None, low, high)
 
     def own(b):
         def body():
@@ -310,7 +307,7 @@
             value = jnp.where(col_of == row_of, value, 2.0 * value)
             main_p[b, 1] = value.astype(main_p.dtype)
             if b == 0:
-                pl.when(further)(lambda: peers(lambda dist: direct_copy(dist, me).start(), 0))
+                pl.when(further)(lambda: direct(0, soon))
             everyone(lambda other: gather_copy(b, other, me, me).start(), None)
         guarded(me, body)
 
@@ -318,6 +315,12 @@
         own(b)
     pl.when(has_after & odd)(corner)
 
+    @pl.when(has_before & even)
+    def _():
+        back.wait_recv()
+        back_s[...] = fold(across(back_v[...], data_v[pl.ds(split, samples - split), pl.ds(0, window)]))
+        everyone(lambda other: back_copy(other, me).start(), None, 0, max(1, count // 2))
+
     @pl.when(odd)
     def _():
         near.wait_recv()
@@ -327,7 +330,9 @@
         near_v[...] = jnp.zeros_like(near_v)
 
     own(blocks - 1)
+    pl.when(further)(lambda: guarded(me, lambda: direct(soon, count)))
     pl.when(has_after & odd)(lambda: everyone(lambda other: late_copy(other, me).start(), False, soon))
+    pl.when(has_before & even)(lambda: everyone(lambda other: back_copy(other, me).start(), None, max(1, count // 2)))
 
     def gathered(b):
         everyone(lambda other: guarded(
@@ -353,7 +358,7 @@
     def sent():
         for b in range(blocks):
             everyone(lambda other: gather_copy(b, other, me, me).wait_send(), None)
-        pl.when(further)(lambda: peers(lambda dist: direct_copy(dist, me).wait_send(), 0))
+        pl.when(further)(lambda: everyone(lambda other: direct_copy(other, me, me).wait_send(), None))
     guarded(me, sent)
 
     gathered(0)
@@ -384,8 +389,8 @@
             corner_out[...] = jnp.where(col < row, beside, 0.0).astype(corner_out.dtype)
             forward.wait_recv()
 
-        pl.when(odd)(lambda: peers(lambda dist: guarded(
-            behind(dist), lambda: direct_copy(dist, behind(dist)).wait_recv()), 0))
+        pl.when(odd)(lambda: everyone(lambda other: guarded(
+            other, lambda: direct_copy(other, other, other).wait_recv()), None))
         far_out[...] = tail_v[...]
 
     @pl.when(jnp.logical_not(has_after))

time: 19.5 us -> 19.5 us (level)
  no operation moved by 1% of the time
where the time goes in v11:
time: 19.5 us; the launch traced here: 19.2 us
  Pallas kernels  19.1 us (98%)
    pallas_call x1, Pallas kernels, reduced_sums(): pl.pallas_call(functools.partial(sums_kernel, count, ring, window), out_s...  17.4 us
    pallas_call x1, Pallas kernels, on_device(): pl.pallas_call(functools.partial(scores_kernel, genotype.shape[0] * lax.a...  1.77 us

profile of v11, /device:TPU:0, one launch (start us, length us, event | category | flops | bytes accessed | tf_op | source)
XLA Modules:
  0.0 19.2 jit_solution(17395044647934559990)
XLA Ops:
  0.0 17.4 %sums.1 = (bf16[2,8,2,16,128]{4,3,2,1,0:T(8,128)(2,1)S(1)}, bf16[8,2,16,128]{3,2,1,0:T(8,128)(2,1)S(1)}, bf16[128,128]{1,0:T(8,128)(2,1)S(1)}, bf16[2,784,256]{2,1,0:T(8,128)(2,1)S(1)}) custom-call(bf16[2048,256]{1,0:T(8,128)(2,1)} %geno.1, f32[16,128]{1,0:T(8,128)} %bitcast.7, f32[16,128]{1,0:T(8,128)} %bitcast.8, s32[2048,127]{1,0:T(8,128)} %flips.1, ...), custom_call_target="tpu_custom_call" | custom-call | tf_op jit(solution)/shard_map/sums/pallas_call | solution.py:452
  17.4 1.8 %scores.1 = f32[49,32,128]{2,1,0:T(8,128)} custom-call(bf16[2,8,2,16,128]{4,3,2,1,0:T(8,128)(2,1)S(1)} %get-tuple-element.9.near, bf16[8,2,16,128]{3,2,1,0:T(8,128)(2,1)S(1)} %get-tuple-element.10.far, bf16[128,128]{1,0:T(8,128)(2,1)S(1)} %get-tuple-element.11.corner, bf16[2,784,256]{2,1,0:T(8,128)(2,1)S(1)} %get-tuple-element.12.placed), custom_call_target="tpu_custom_call" | custom-call | tf_op jit(solution)/shard_map/scores/pallas_call | solution.py:543
